TPU v7x, 128 devices: a whole 4x4x4 slice. The times are simulated.
128 devices in a mesh: fsdp: 32 (over z, x, core), tensor: 4 (over y).
Axes of the slice: x: 4, y: 4, z: 4, core: 2. Of those that a mesh axis runs over, the one named last changes fastest.
Arguments:
- hidden: bfloat16 [512, 28672], P('tensor', 'fsdp'), may hold values from -6 to 6
- down_weight: bfloat16 [28672, 16384], P('fsdp', 'tensor'), may hold values from -0.03125 to 0.03125
- covariance: float32 [16384, 16384], P('tensor', 'fsdp'), as said below
- keep_index: int32 [32, 8], P('fsdp'), may hold values from -1 to 15, as said below
- start_basis: float32 [16384, 512], P('fsdp'), may hold values from -6 to 6
Outputs:
- mlp_out: bfloat16 [512, 16384], P('fsdp', 'tensor')
- new_covariance: float32 [16384, 16384], P('tensor', 'fsdp')
- first_basis: float32 [16384, 512], P(('tensor', 'fsdp'))
- final_basis: float32 [16384, 512], P('fsdp')
Inputs may be any that keep to these rules, and one draw needn't show every extreme that they name: `keep_index`: row b lists first between 1 and 8 distinct positions of 0 to 15, then -1 in the remaining slots; in every draw some row lists 8 positions. covariance is exactly symmetric and positive definite.
All inputs are finite; a program needn't handle non-finite values.
Results may differ from a plain program's by a relative error of at most 0.0015.
Values may be sent and summed in bfloat16 or wider, within the bound.
A program may use at most 128 MiB of HBM per device.

v0:
```python
import math

import jax
import jax.numpy as jnp
from jax import lax
from jax.sharding import PartitionSpec as P

D = 16384
TOK_DEV = 16


def broadcast(x, axis, root):
    mine = lax.axis_index(axis) == root
    return lax.psum(jnp.where(mine, x, jnp.zeros_like(x)), axis)


def gram_local(image_rows):
    return jnp.dot(
        image_rows.T,
        image_rows,
        precision=lax.Precision.HIGHEST,
        preferred_element_type=jnp.float32,
    )


def solve_rows(image_rows, lower_factor):
    return jax.scipy.linalg.solve_triangular(lower_factor, image_rows.T, lower=True).T


def body(hidden, down_weight, covariance, keep_index, start_basis):
    highest = lax.Precision.HIGHEST
    fsdp_count = lax.axis_size("fsdp")
    total_tokens = TOK_DEV * fsdp_count
    quarter = covariance.shape[0]
    block_width = covariance.shape[1]
    share_rows = quarter // fsdp_count
    group_size = fsdp_count // lax.axis_size("tensor")
    all_hidden = lax.all_gather(hidden, "tensor", axis=0, tiled=True)
    mlp_out = lax.psum_scatter(
        jnp.dot(all_hidden, down_weight, preferred_element_type=jnp.float32),
        "fsdp",
        scatter_dimension=0,
        tiled=True,
    ).astype(jnp.bfloat16)
    listed = keep_index[0]
    fsdp_index = lax.axis_index("fsdp")
    col_offset = fsdp_index % group_size * block_width
    source_index = fsdp_index // group_size
    positions = jnp.arange(mlp_out.shape[0], dtype=jnp.int32)
    marked = jnp.any(listed[:, None] == positions[None, :], axis=0).astype(jnp.bfloat16)
    row_data = lax.all_gather(mlp_out * marked[:, None], "fsdp", axis=0, tiled=True)
    column_data = broadcast(
        lax.dynamic_slice_in_dim(row_data, col_offset, block_width, 1), "tensor", source_index
    )
    update = lax.dot_general(
        row_data, column_data, (((0,), (0,)), ((), ())), preferred_element_type=jnp.float32
    )
    new_covariance = covariance + update * (1.0 / total_tokens)
    partial_image = jnp.dot(
        new_covariance, start_basis, precision=highest, preferred_element_type=jnp.float32
    )
    first_image = lax.psum(partial_image, "fsdp")
    first_gram = lax.psum(gram_local(first_image), "tensor")
    own_image = lax.dynamic_slice_in_dim(first_image, fsdp_index * share_rows, share_rows, 0)
    first_factor = jnp.linalg.cholesky(first_gram)
    first_basis = solve_rows(own_image, first_factor) * math.sqrt(D)
    carried = solve_rows(first_image, first_factor)
    partial_second = lax.dot_general(
        new_covariance,
        carried,
        (((0,), (0,)), ((), ())),
        precision=highest,
        preferred_element_type=jnp.float32,
    )
    second = lax.psum(partial_second, "tensor")
    second_gram = lax.psum(gram_local(second), "fsdp")
    final_basis = solve_rows(second, jnp.linalg.cholesky(second_gram)) * math.sqrt(D)
    return (mlp_out, new_covariance, first_basis, final_basis)


def solution(mesh):
    placed = (
        P("tensor", "fsdp"),
        P("fsdp", "tensor"),
        P("tensor", "fsdp"),
        P("fsdp", None),
        P("fsdp", None),
    )
    return jax.shard_map(
        body,
        mesh=mesh,
        in_specs=placed,
        out_specs=(
            P("fsdp", "tensor"),
            P("tensor", "fsdp"),
            P(("tensor", "fsdp"), None),
            P("fsdp", None),
        ),
        check_vma=False,
    )
```

profile of v0, /device:TPU:1, one launch (start us, length us, event | category | flops | bytes accessed | tf_op | source)
XLA Modules:
  0.0 948.6 jit_solution(741812926708005223)
XLA Ops:
  7.2 14.1 %all_gather.6 = bf16[512,896]{1,0:T(8,128)(2,1)S(1)} all-gather(bf16[128,896]{1,0:T(8,128)(2,1)} %param.6), channel_id=1, replica_groups=mesh['fsdp'=32,'tensor'=4] {'tensor'}, dimensions={0}, use_global_device_ids=true | all-gather | bytes 1146880 | tf_op jit(solution)/shard_map/all_gather | solution.py:38
  31.8 94.6 %reduce-scatter.2.cloned.1.call-done = f32[16,4096]{1,0:T(8,128)} async-done(((f32[512,4096]{1,0:T(8,128)}), f32[16,4096]{1,0:T(8,128)}) %reduce-scatter.2.cloned.1.call-update) | async-done | bytes 262160 | tf_op jit(solution)/shard_map/reduce_scatter | solution.py:39
  128.2 48.6 %all-gather.2.cloned.1.call-done = bf16[512,4096]{1,0:T(8,128)(2,1)} async-done(((bf16[16,4096]{1,0:T(8,128)(2,1)}), bf16[512,4096]{1,0:T(8,128)(2,1)}) %all-gather.2.cloned.1.call-update) | async-done | bytes 4194320 | tf_op jit(solution)/shard_map/all_gather | solution.py:51
  178.8 40.7 %all-reduce.7.cloned.1.call-done = bf16[512,512]{1,0:T(8,128)(2,1)} async-done(((bf16[512,512]{1,0:T(8,128)(2,1)}), bf16[512,512]{1,0:T(8,128)(2,1)}) %all-reduce.7.cloned.1.call-update) | async-done | bytes 524304 | tf_op jit(solution)/shard_map/psum | solution.py:14
  230.3 15.7 %fusion.97 = f32[4096,512]{1,0:T(8,128)} fusion(f32[4096,512]{1,0:T(8,128)S(1)} %multiply_add_fusion, f32[512,512]{1,0:T(8,128)S(1)} %copy-done), kind=kOutput, calls=%fused_computation.170 | convolution fusion | flops 12884901888 | bytes 17825792 | tf_op jit(solution)/shard_map/dot_general | solution.py:59
  246.4 122.9 %all-reduce.9.cloned.1.call-done = f32[4096,512]{1,0:T(8,128)} async-done(((f32[4096,512]{1,0:T(8,128)}), f32[4096,512]{1,0:T(8,128)}) %all-reduce.9.cloned.1.call-update) | async-done | bytes 8388624 | tf_op jit(solution)/shard_map/psum | solution.py:62
  369.2 18.5 %fusion.98 = f32[512,512]{0,1:T(8,128)} fusion(f32[4096,512]{1,0:T(8,128)} %all-reduce.9.cloned.1.call-done), kind=kOutput, calls=%fused_computation.171 | convolution fusion | flops 12884901888 | bytes 9437184 | tf_op jit(solution)/shard_map/dot_general | solution.py:18
  388.8 43.1 %all-reduce.11.cloned.1.call-done = f32[512,512]{0,1:T(8,128)} async-done(((f32[512,512]{0,1:T(8,128)}), f32[512,512]{0,1:T(8,128)}) %all-reduce.11.cloned.1.call-update) | async-done | bytes 1048592 | tf_op jit(solution)/shard_map/psum | solution.py:63
  434.9 11.7 %cholesky.286 = f32[128,128]{1,0:T(8,128)S(1)} custom-call(f32[128,128]{1,0:T(8,128)S(1)} %cholesky.426), custom_call_target="Cholesky" | custom-call | tf_op jit(solution)/shard_map/jit(cholesky)/cholesky | solution.py:65
  457.3 11.7 %cholesky.305 = f32[128,128]{1,0:T(8,128)S(1)} custom-call(f32[128,128]{1,0:T(8,128)S(1)} %cholesky.430), custom_call_target="Cholesky" | custom-call | tf_op jit(solution)/shard_map/jit(cholesky)/cholesky | solution.py:65
  469.0 18.5 %custom-call.37 = f32[1,128,128]{1,2,0:T(8,128)S(1)} custom-call(f32[1,128,128]{2,1,0:T(8,128)S(1)} %get-tuple-element.67), custom_call_target="InvertDiagBlocksLowerTriangular" | custom-call | tf_op jit(solution)/shard_map/jit(cholesky)/cholesky | solution.py:65
  488.2 11.7 %cholesky.326 = f32[128,128]{1,0:T(8,128)S(1)} custom-call(f32[128,128]{1,0:T(8,128)S(1)} %cholesky.435), custom_call_target="Cholesky" | custom-call | tf_op jit(solution)/shard_map/jit(cholesky)/cholesky | solution.py:65
  510.4 11.7 %cholesky.343 = f32[128,128]{1,0:T(8,128)S(1)} custom-call(f32[128,128]{1,0:T(8,128)S(1)} %convolution_subtract_fusion.13), custom_call_target="Cholesky" | custom-call | tf_op jit(solution)/shard_map/jit(cholesky)/cholesky | solution.py:65
  535.1 39.3 %custom-call.31 = f32[4,128,128]{1,2,0:T(8,128)S(1)} custom-call(f32[4,128,128]{2,1,0:T(8,128)S(1)} %get-tuple-element.12), custom_call_target="InvertDiagBlocksLowerTriangular" | custom-call | tf_op jit(solution)/shard_map/jit(_solve_triangular)/triangular_solve | solution.py:27
  595.9 12.4 %fusion.14 = f32[128,4096]{0,1:T(8,128)S(1)} fusion(f32[128,4096]{1,0:T(8,128)S(1)} %fusion.80, f32[128,4096]{1,0:T(8,128)S(1)} %fusion.78, f32[128,4096]{1,0:T(8,128)S(1)} %fusion.20, f32[512,4096]{0,1:T(8,128)} %bitcast.127, f32[512,512]{1,0:T(8,128)S(1)} %get-tuple-element.179), kind=kOutput, calls=%fused_computation.21 | convolution fusion | flops 2419589120 | bytes 10682368 | tf_op jit(solution)/shard_map/jit(_solve_triangular)/triangular_solve | solution.py:27
  610.3 29.5 %fusion = f32[512,512]{1,0:T(8,128)} fusion(f32[4096,512]{1,0:T(8,128)S(1)} %bitcast.129, f32[128,4096]{1,0:T(8,128)S(1)} %fusion.82, f32[128,4096]{1,0:T(8,128)S(1)} %fusion.80, f32[128,4096]{1,0:T(8,128)S(1)} %fusion.78, f32[128,4096]{1,0:T(8,128)S(1)} %fusion.20), kind=kOutput, calls=%fused_computation.4 | convolution fusion | flops 12891193344 | bytes 17825792 | tf_op jit(solution)/shard_map/dot_general | solution.py:68
  641.5 45.5 %all-reduce.13.cloned.1.call-done = f32[512,512]{1,0:T(8,128)} async-done(((f32[512,512]{1,0:T(8,128)}), f32[512,512]{1,0:T(8,128)}) %all-reduce.13.cloned.1.call-update) | async-done | bytes 1048592 | tf_op jit(solution)/shard_map/psum | solution.py:75
  693.1 106.8 %all-reduce.15.cloned.1.call-done = f32[512,512]{0,1:T(8,128)} async-done(((f32[512,512]{0,1:T(8,128)}), f32[512,512]{0,1:T(8,128)}) %all-reduce.15.cloned.1.call-update) | async-done | bytes 1048592 | tf_op jit(solution)/shard_map/psum | solution.py:76
  802.9 11.7 %cholesky.358 = f32[128,128]{1,0:T(8,128)S(1)} custom-call(f32[128,128]{1,0:T(8,128)S(1)} %cholesky.439), custom_call_target="Cholesky" | custom-call | tf_op jit(solution)/shard_map/jit(cholesky)/cholesky | solution.py:77
  825.3 11.9 %cholesky.377 = f32[128,128]{1,0:T(8,128)S(1)} custom-call(f32[128,128]{1,0:T(8,128)S(1)} %cholesky.443), custom_call_target="Cholesky" | custom-call | tf_op jit(solution)/shard_map/jit(cholesky)/cholesky | solution.py:77
  837.2 9.8 %custom-call.40 = f32[1,128,128]{1,2,0:T(8,128)S(1)} custom-call(f32[1,128,128]{2,1,0:T(8,128)S(1)} %get-tuple-element.57), custom_call_target="InvertDiagBlocksLowerTriangular" | custom-call | tf_op jit(solution)/shard_map/jit(cholesky)/cholesky | solution.py:77
  847.7 11.7 %cholesky.398 = f32[128,128]{1,0:T(8,128)S(1)} custom-call(f32[128,128]{1,0:T(8,128)S(1)} %cholesky.448), custom_call_target="Cholesky" | custom-call | tf_op jit(solution)/shard_map/jit(cholesky)/cholesky | solution.py:77
  869.9 11.9 %cholesky.415 = f32[128,128]{1,0:T(8,128)S(1)} custom-call(f32[128,128]{1,0:T(8,128)S(1)} %convolution_subtract_fusion.11), custom_call_target="Cholesky" | custom-call | tf_op jit(solution)/shard_map/jit(cholesky)/cholesky | solution.py:77
  895.7 39.3 %custom-call.32 = f32[4,128,128]{1,2,0:T(8,128)S(1)} custom-call(f32[4,128,128]{2,1,0:T(8,128)S(1)} %get-tuple-element.20), custom_call_target="InvertDiagBlocksLowerTriangular" | custom-call | tf_op jit(solution)/shard_map/jit(_solve_triangular)/triangular_solve | solution.py:27
  (136 shorter events, 151.3 us)
Async XLA Ops:
  7.2 223.2 %copy-start = (f32[512,512]{1,0:T(8,128)S(1)}, f32[512,512]{1,0:T(8,128)}, u32[]{:S(2)}) copy-start(f32[512,512]{1,0:T(8,128)} %param.10) | copy-start | bytes 3145732
  7.2 119.2 %reduce-scatter.2.cloned.1.call-start = ((), (), s32[]{:S(2)}) async-start(), calls=%async_computation.1 | async-start | bytes 8650752 | tf_op jit(solution)/shard_map/reduce_scatter | solution.py:39
  31.1 0.7 copy-start.4
  31.1 145.6 %all-gather.2.cloned.1.call-start = ((), (), s32[]{:S(2)}) async-start(), calls=%async_computation.2 | async-start | bytes 4325376 | tf_op jit(solution)/shard_map/all_gather | solution.py:51
  128.1 91.4 %all-reduce.7.cloned.1.call-start = ((), (), s32[]{:S(2)}) async-start(), calls=%async_computation.3 | async-start | bytes 1048576 | tf_op jit(solution)/shard_map/psum | solution.py:14
  178.7 190.5 %all-reduce.9.cloned.1.call-start = ((), (), s32[]{:S(2)}) async-start(), calls=%async_computation.4 | async-start | bytes 16777216 | tf_op jit(solution)/shard_map/psum | solution.py:62
  226.9 3.4 copy-start.2
  246.1 185.8 %all-reduce.11.cloned.1.call-start = ((), (), s32[]{:S(2)}) async-start(), calls=%async_computation.5 | async-start | bytes 2097152 | tf_op jit(solution)/shard_map/psum | solution.py:63
  387.7 299.3 %all-reduce.13.cloned.1.call-start = ((), (), s32[]{:S(2)}) async-start(), calls=%async_computation.6 | async-start | bytes 2097152 | tf_op jit(solution)/shard_map/psum | solution.py:75
  593.9 16.4 %slice-start = ((s8[8388608]{0:T(1024)(128)(4,1)}), s8[4194304]{0:T(1024)(128)(4,1)S(1)}, s32[]{:S(2)}) async-start(s8[8388608]{0:T(1024)(128)(4,1)} %bitcast.128), calls=%async_computation.8 | async-start | bytes 8388608
  595.9 14.4 %slice-start.1 = ((s8[8388608]{0:T(1024)(128)(4,1)}), s8[4194304]{0:T(1024)(128)(4,1)S(1)}, s32[]{:S(2)}) async-start(s8[8388608]{0:T(1024)(128)(4,1)} %bitcast.128), calls=%async_computation.9 | async-start | bytes 8388608
  639.9 160.0 %all-reduce.15.cloned.1.call-start = ((), (), s32[]{:S(2)}) async-start(), calls=%async_computation.7 | async-start | bytes 2097152 | tf_op jit(solution)/shard_map/psum | solution.py:76
  802.9 132.1 %copy-start.3 = (f32[512,512]{1,0:T(8,128)S(1)}, f32[512,512]{1,0:T(8,128)}, u32[]{:S(2)}) copy-start(f32[512,512]{1,0:T(8,128)} %all-reduce.13.cloned.1.call-done) | copy-start | bytes 3145732
  935.5 5.8 copy-start.1
Sparse Core Ops, SparseCore 0:
  31.2 95.1 reduce-scatter.1
  129.2 47.4 all-gather.1
  179.7 39.7 all-reduce.6
  246.2 122.9 all-reduce.8
  387.9 43.9 all-reduce.10
  640.0 46.9 all-reduce.12
  691.5 108.3 all-reduce.14
where the time goes:
time: 957 us; the launch traced here: 949 us
  waiting for transfers between devices  502 us (52%)
  other arithmetic  253 us (26%)
  matrix products  132 us (14%)
  local copies, waits for them, and re-layouts  26.9 us (3%)
  between operations  20.2 us (2%)
  blocking collectives  14.1 us (1%)
    psum x1, waiting for transfers between devices, body(): first_image = lax.psum(partial_image, 'fsdp')  123 us
    psum x1, waiting for transfers between devices, body(): second_gram = lax.psum(gram_local(second), 'fsdp')  107 us
    reduce_scatter x1, waiting for transfers between devices, body(): lax.psum_scatter(jnp.dot(all_hidden, down_weight, preferred_element_type=...  94.6 us
    another operation x14, other arithmetic, body(): first_factor = jnp.linalg.cholesky(first_gram)  87 us
    another operation x15, other arithmetic, body(): jnp.linalg.cholesky(second_gram)  79.5 us
    another operation x5, other arithmetic, solve_rows(): jax.scipy.linalg.solve_triangular(lower_factor, image_rows.T, lower=True)  79.3 us
    all_gather x1, waiting for transfers between devices, body(): lax.all_gather(mlp_out * marked[:, None], 'fsdp', axis=0, tiled=True)  48.6 us
    psum x1, waiting for transfers between devices, body(): second = lax.psum(partial_second, 'tensor')  45.5 us
  transfers between devices with their start and end apart: 7, of which 7 were waited for; matrix products, arithmetic and copies ran while one was open for 0% of the time, Pallas kernels for 0%

commit v1 on v0

v1 whole, which is shorter than its diff:
```python
import functools
import math

import jax
import jax.numpy as jnp
from jax import lax
from jax.experimental import pallas as pl
from jax.experimental.pallas import tpu as pltpu
from jax.sharding import PartitionSpec as P

D = 16384
TOK_DEV = 16
F32 = jnp.float32
BF16 = jnp.bfloat16
HIGH = lax.Precision.HIGH


def inverse_factor_kernel(gram_ref, out_ref, scaled, work, state):
    n = gram_ref.shape[0]
    rows = lax.broadcasted_iota(jnp.int32, (n, n), 0)
    cols = lax.broadcasted_iota(jnp.int32, (n, n), 1)
    gram = gram_ref[...]
    diagonal = jnp.where(rows == cols, gram, 0.0)
    col_scale = lax.rsqrt(jnp.sum(diagonal, axis=1, keepdims=True))
    row_scale = lax.rsqrt(jnp.sum(diagonal, axis=0, keepdims=True))
    scaled[...] = gram * col_scale * row_scale

    def half_lower(residual):
        return jnp.where(rows > cols, residual, jnp.where(rows == cols, 0.5 * residual, 0.0))

    def residual_of(x, precision):
        left = jnp.dot(x, scaled[...], precision=precision, preferred_element_type=F32)
        full = lax.dot_general(
            left, x, (((1,), (1,)), ((), ())), precision=precision, preferred_element_type=F32
        )
        return full - jnp.where(rows == cols, 1.0, 0.0)

    eye = jnp.where(rows == cols, 1.0, 0.0)
    work[...] = eye - half_lower(scaled[...] - eye)

    @pl.loop(0, 3)
    def _(step):
        x = work[...]
        residual = residual_of(x, None)
        work[...] = x - jnp.dot(half_lower(residual), x, preferred_element_type=F32)

    state[0] = 1.0

    def unfinished(step):
        error = state[0]
        return jnp.logical_and(step < 12, jnp.logical_not(error < 1e-5))

    def refine(step):
        x = work[...]
        residual = residual_of(x, HIGH)
        work[...] = x - jnp.dot(half_lower(residual), x, precision=HIGH, preferred_element_type=F32)
        state[0] = jnp.sum(residual * residual)
        return step + 1

    lax.while_loop(unfinished, refine, 0)

    @pl.when(jnp.logical_not(state[0] < 1e-5))
    def _():
        work[...] = eye

        @pl.loop(0, n)
        def _(j):
            here = cols[0:1] == j
            pivot_row = scaled[pl.ds(j, 1), :]
            pivot = lax.rsqrt(jnp.sum(jnp.where(here, pivot_row, 0.0), axis=1, keepdims=True))
            left = jnp.sum(jnp.where(cols == j, scaled[...], 0.0), axis=1, keepdims=True) * pivot
            left = jnp.where(rows[:, 0:1] > j, left, 0.0)
            own = work[pl.ds(j, 1), :] * pivot
            scaled[...] = scaled[...] - left * (pivot_row * pivot)
            work[...] = work[...] - left * own
            work[pl.ds(j, 1), :] = own

    out_ref[...] = work[...] * row_scale


def inverse_factor(gram):
    n = gram.shape[0]
    return pl.pallas_call(
        inverse_factor_kernel,
        out_shape=jax.ShapeDtypeStruct((n, n), F32),
        in_specs=[pl.BlockSpec(memory_space=pltpu.VMEM)],
        out_specs=pl.BlockSpec(memory_space=pltpu.VMEM),
        scratch_shapes=[pltpu.VMEM((n, n), F32), pltpu.VMEM((n, n), F32), pltpu.SMEM((1,), F32)],
        cost_estimate=pl.CostEstimate(flops=8_000_000_000, bytes_accessed=2 << 20, transcendentals=0),
        name="inverse_factor",
    )(gram)


def times_transpose(rows, factor, scale=1.0):
    out = lax.dot_general(
        rows, factor, (((1,), (1,)), ((), ())), precision=HIGH, preferred_element_type=F32
    )
    return out * scale if scale != 1.0 else out


def gram_of(rows):
    return lax.dot_general(
        rows, rows, (((0,), (0,)), ((), ())), precision=HIGH, preferred_element_type=F32
    )


def swap_axes(share, planes, group):
    perm = [
        ((z * group + r) * planes + t, (t * group + r) * planes + z)
        for z in range(planes)
        for r in range(group)
        for t in range(planes)
    ]
    return lax.ppermute(share, ("fsdp", "tensor"), perm)


def spread(share, planes, group):
    moved = swap_axes(share, planes, group)
    whole = lax.all_gather(moved, "fsdp", axis=0)
    rows, width = share.shape
    return whole.reshape(planes, group, rows, width).transpose(1, 0, 2, 3).reshape(-1, width)


def body(hidden, down_weight, covariance, keep_index, start_basis):
    fsdp_count = lax.axis_size("fsdp")
    planes = lax.axis_size("tensor")
    group = fsdp_count // planes
    total_tokens = TOK_DEV * fsdp_count
    quarter, block_width = covariance.shape
    share_rows = quarter // fsdp_count
    f = lax.axis_index("fsdp")
    t = lax.axis_index("tensor")
    root = math.sqrt(D)

    start_share = lax.dynamic_slice_in_dim(start_basis, t * share_rows, share_rows, 0)
    start_rows = spread(start_share, planes, group)

    all_hidden = lax.all_gather(hidden, "tensor", axis=0, tiled=True)
    mlp_out = lax.psum_scatter(
        jnp.dot(all_hidden, down_weight, preferred_element_type=F32),
        "fsdp",
        scatter_dimension=0,
        tiled=True,
    ).astype(BF16)
    listed = keep_index[0]
    positions = jnp.arange(mlp_out.shape[0], dtype=jnp.int32)
    chosen = (listed[:, None] == positions[None, :]).astype(BF16)
    kept = jnp.dot(chosen, mlp_out, preferred_element_type=F32).astype(BF16)
    kept_rows = lax.all_gather(kept, "fsdp", axis=0, tiled=True)
    own = lax.dynamic_slice_in_dim(kept_rows, f % group * block_width, block_width, 1)
    kept_cols = lax.psum(jnp.where(t == f // group, own, jnp.zeros_like(own)), "tensor")
    update = lax.dot_general(
        kept_rows, kept_cols, (((0,), (0,)), ((), ())), preferred_element_type=F32
    )
    new_covariance = covariance + update * (1.0 / total_tokens)

    def image_share(rows):
        partial = lax.dot_general(
            new_covariance, rows, (((0,), (0,)), ((), ())), precision=HIGH, preferred_element_type=F32
        )
        return lax.psum_scatter(partial, "tensor", scatter_dimension=0, tiled=True)

    image_one = image_share(start_rows)
    image_rows = spread(image_one, planes, group)
    inverse_one = inverse_factor(lax.psum(gram_of(image_one), ("fsdp", "tensor")))
    own_rows = lax.dynamic_slice_in_dim(image_rows, f * share_rows, share_rows, 0)
    first_basis = times_transpose(own_rows, inverse_one, root)
    image_two = times_transpose(image_share(image_rows), inverse_one)
    whole_two = lax.all_gather(image_two, "tensor", axis=0, tiled=True)
    inverse_two = inverse_factor(lax.psum(gram_of(image_two), ("fsdp", "tensor")))
    final_basis = times_transpose(whole_two, inverse_two, root)
    return (mlp_out, new_covariance, first_basis, final_basis)


def solution(mesh):
    placed = (
        P("tensor", "fsdp"),
        P("fsdp", "tensor"),
        P("tensor", "fsdp"),
        P("fsdp", None),
        P("fsdp", None),
    )
    return jax.shard_map(
        body,
        mesh=mesh,
        in_specs=placed,
        out_specs=(
            P("fsdp", "tensor"),
            P("tensor", "fsdp"),
            P(("tensor", "fsdp"), None),
            P("fsdp", None),
        ),
        check_vma=False,
    )
```

time: 957 us -> 908 us (0.949)
  other arithmetic: 253 us -> 2.66 us
  Pallas kernels: 0 us -> 196 us
  waiting for transfers between devices: 502 us -> 609 us
  matrix products: 132 us -> 46.2 us
    another operation x34 -> x0, other arithmetic: 246 us -> none  [the longest x14 87 us: body(): first_factor = jnp.linalg.cholesky(first_gram)]
    pallas_call x0 -> x2, Pallas kernels: none -> 196 us  [inverse_factor(): pl.pallas_call(inverse_factor_kernel, out_shape=jax.ShapeDtypeStruct((n,...]
    all_gather x1 -> x4, waiting for transfers between devices: 48.6 us -> 176 us  [the longest x2 120 us: spread(): whole = lax.all_gather(moved, 'fsdp', axis=0)]
    psum x5 -> x3, waiting for transfers between devices: 359 us -> 311 us  [the longest x1 144 us: body(): lax.psum(gram_of(image_two), ('fsdp', 'tensor'))]
    another operation x33 -> x0, matrix products: 46.6 us -> none  [the longest x21 42.9 us: solve_rows(): jax.scipy.linalg.solve_triangular(lower_factor, image_rows.T, lower=True)]
    dot_general x6 -> x10, matrix products: 85.3 us -> 46.2 us  [the longest x2 18.3 us: image_share(): lax.dot_general(new_covariance, rows, (((0,), (0,)), ((), ())), precision...]
    reduce_scatter x0 -> x2, waiting for transfers between devices: none -> 25 us  [image_share(): return lax.psum_scatter(partial, 'tensor', scatter_dimension=0, tiled=True)]
    another operation x33 -> x0, local copies, waits for them, and re-layouts: 16.6 us -> none
  transfers between devices with their start and end apart: 7 -> 12, of which waited for: 7 -> 9; matrix products, arithmetic and copies ran while one was open for 0% -> 3% of each run, Pallas kernels for 0% -> 22%
where the time goes in v1:
time: 908 us; the launch traced here: 906 us
  waiting for transfers between devices  609 us (67%)
  Pallas kernels  196 us (22%)
  matrix products  46.2 us (5%)
  local copies, waits for them, and re-layouts  20.9 us (2%)
  between operations  14.3 us (2%)
  blocking collectives  14.1 us (2%)
    pallas_call x2, Pallas kernels, inverse_factor(): pl.pallas_call(inverse_factor_kernel, out_shape=jax.ShapeDtypeStruct((n,...  196 us
    psum x1, waiting for transfers between devices, body(): lax.psum(gram_of(image_two), ('fsdp', 'tensor'))  144 us
    psum x1, waiting for transfers between devices, body(): lax.psum(gram_of(image_one), ('fsdp', 'tensor'))  135 us
    all_gather x2, waiting for transfers between devices, spread(): whole = lax.all_gather(moved, 'fsdp', axis=0)  120 us
    reduce_scatter x1, waiting for transfers between devices, body(): lax.psum_scatter(jnp.dot(all_hidden, down_weight, preferred_element_type=...  95.2 us
    all_gather x1, waiting for transfers between devices, body(): kept_rows = lax.all_gather(kept, 'fsdp', axis=0, tiled=True)  45.8 us
    psum x1, waiting for transfers between devices, body(): lax.psum(jnp.where(t == f // group, own, jnp.zeros_like(own)), 'tensor')  33.2 us
    reduce_scatter x2, waiting for transfers between devices, image_share(): return lax.psum_scatter(partial, 'tensor', scatter_dimension=0, tiled=True)  25 us
  transfers between devices with their start and end apart: 12, of which 9 were waited for; matrix products, arithmetic and copies ran while one was open for 3% of the time, Pallas kernels for 22%

profile of v1, /device:TPU:1, one launch (start us, length us, event | category | flops | bytes accessed | tf_op | source)
XLA Modules:
  0.0 906.4 jit_solution(4333567180382945393)
XLA Ops:
  7.2 14.1 %all_gather.21 = bf16[512,896]{1,0:T(8,128)(2,1)S(1)} all-gather(bf16[128,896]{1,0:T(8,128)(2,1)} %param.5), channel_id=1, replica_groups=mesh['fsdp'=32,'tensor'=4] {'tensor'}, dimensions={0}, use_global_device_ids=true | all-gather | bytes 1146880 | tf_op jit(solution)/shard_map/all_gather | solution.py:138
  21.3 9.8 %fusion.3 = f32[512,4096]{1,0:T(8,128)} fusion(bf16[512,896]{1,0:T(8,128)(2,1)S(1)} %all_gather.21, bf16[896,4096]{1,0:T(8,128)(2,1)} %param.6), kind=kOutput, calls=%fused_computation.10 | convolution fusion | flops 3758096384 | bytes 16646144 | tf_op jit(solution)/shard_map/dot_general | solution.py:140
  31.2 95.2 %reduce-scatter.4.cloned.1.call-done = f32[16,4096]{1,0:T(8,128)} async-done(((f32[512,4096]{1,0:T(8,128)}), f32[16,4096]{1,0:T(8,128)}) %reduce-scatter.4.cloned.1.call-update) | async-done | bytes 262160 | tf_op jit(solution)/shard_map/reduce_scatter | solution.py:139
  129.9 45.8 %all-gather.7.cloned.1.call-done = bf16[256,4096]{1,0:T(8,128)(2,1)} async-done(((bf16[8,4096]{1,0:T(8,128)(2,1)}), bf16[256,4096]{1,0:T(8,128)(2,1)}) %all-gather.7.cloned.1.call-update) | async-done | bytes 2097168 | tf_op jit(solution)/shard_map/all_gather | solution.py:149
  177.6 53.1 %all-gather.11.cloned.1.call-done = f32[4096,512]{1,0:T(8,128)} async-done(((f32[128,512]{1,0:T(8,128)}), f32[4096,512]{1,0:T(8,128)}) %all-gather.11.cloned.1.call-update) | async-done | bytes 8388624 | tf_op jit(solution)/shard_map/all_gather | solution.py:119
  230.7 8.4 copy.10
  239.0 33.2 %all-reduce.4.cloned.1.call-done = bf16[256,512]{1,0:T(8,128)(2,1)} async-done(((bf16[256,512]{1,0:T(8,128)(2,1)}), bf16[256,512]{1,0:T(8,128)(2,1)}) %all-reduce.4.cloned.1.call-update) | async-done | bytes 262160 | tf_op jit(solution)/shard_map/psum | solution.py:151
  272.2 4.9 multiply_add_fusion
  277.2 3.4 copy-done.2
  280.5 7.7 fusion.4
  288.3 25.0 %reduce-scatter.6.cloned.1.call-done = f32[128,512]{1,0:T(8,128)} async-done(((f32[512,512]{1,0:T(8,128)}), f32[128,512]{1,0:T(8,128)}) %reduce-scatter.6.cloned.1.call-update) | async-done | bytes 262160 | tf_op jit(solution)/shard_map/reduce_scatter | solution.py:161
  315.6 2.6 fusion.5
  318.6 66.5 %all-gather.13.cloned.1.call-done = f32[4096,512]{1,0:T(8,128)} async-done(((f32[128,512]{1,0:T(8,128)}), f32[4096,512]{1,0:T(8,128)}) %all-gather.13.cloned.1.call-update) | async-done | bytes 8388624 | tf_op jit(solution)/shard_map/all_gather | solution.py:119
  385.1 4.4 copy.11
  389.5 3.3 copy-done.3
  392.7 10.6 %fusion.6 = f32[512,512]{1,0:T(8,128)} fusion(f32[4096,512]{1,0:T(8,128)} %copy-done.2, f32[4096,512]{1,0:T(8,128)S(1)} %bitcast.27), kind=kOutput, calls=%fused_computation.13 | convolution fusion | flops 6442450944 | bytes 17825792 | tf_op jit(solution)/shard_map/dot_general | solution.py:158
  403.4 134.5 %all-reduce.6.cloned.1.call-done.gram_ref = f32[512,512]{1,0:T(8,128)} async-done(((f32[512,512]{1,0:T(8,128)}), f32[512,512]{1,0:T(8,128)}) %all-reduce.6.cloned.1.call-update) | async-done | bytes 1048592 | tf_op jit(solution)/shard_map/psum | solution.py:165
  538.0 185.3 %inverse_factor.2 = f32[512,512]{1,0:T(8,128)} custom-call(f32[512,512]{1,0:T(8,128)} %all-reduce.6.cloned.1.call-done.gram_ref), custom_call_target="tpu_custom_call" | custom-call | flops 8000000000 | bytes 2097152 | tf_op jit(solution)/shard_map/inverse_factor/pallas_call | solution.py:83
  723.3 2.0 fusion.7
  727.5 2.7 convolution_multiply_fusion.1
  730.2 143.7 %all-reduce.8.cloned.1.call-done.gram_ref = f32[512,512]{1,0:T(8,128)} async-done(((f32[512,512]{1,0:T(8,128)}), f32[512,512]{1,0:T(8,128)}) %all-reduce.8.cloned.1.call-update) | async-done | bytes 1048592 | tf_op jit(solution)/shard_map/psum | solution.py:170
  873.9 11.1 %inverse_factor.3 = f32[512,512]{1,0:T(8,128)} custom-call(f32[512,512]{1,0:T(8,128)} %all-reduce.8.cloned.1.call-done.gram_ref), custom_call_target="tpu_custom_call" | custom-call | flops 8000000000 | bytes 2097152 | tf_op jit(solution)/shard_map/inverse_factor/pallas_call | solution.py:83
  885.0 11.0 %all-gather.9.cloned.1.call-done = f32[512,512]{1,0:T(8,128)} async-done(((f32[128,512]{1,0:T(8,128)}), f32[512,512]{1,0:T(8,128)}) %all-gather.9.cloned.1.call-update) | async-done | bytes 1048592 | tf_op jit(solution)/shard_map/all_gather | solution.py:169
  896.0 3.5 convolution_multiply_fusion
  (50 shorter events, 10.3 us)
Async XLA Ops:
  7.2 121.2 %copy-start = (f32[512,512]{1,0:T(8,128)S(1)}, f32[512,512]{1,0:T(8,128)}, u32[]{:S(2)}) copy-start(f32[512,512]{1,0:T(8,128)} %param.9) | copy-start | bytes 3145732
  7.2 119.2 %reduce-scatter.4.cloned.1.call-start = ((), (), s32[]{:S(2)}) async-start(), calls=%async_computation.3 | async-start | bytes 8650752 | tf_op jit(solution)/shard_map/reduce_scatter | solution.py:139
  31.1 96.3 %copy-start.10 = (s32[1,8]{1,0:T(1,128)S(1)}, s32[1,8]{1,0:T(1,128)}, u32[]{:S(2)}) copy-start(s32[1,8]{1,0:T(1,128)} %param.8) | copy-start | bytes 100
  31.1 144.5 %all-gather.7.cloned.1.call-start = ((), (), s32[]{:S(2)}) async-start(), calls=%async_computation.4 | async-start | bytes 2162688 | tf_op jit(solution)/shard_map/all_gather | solution.py:149
  127.4 111.7 %copy-start.7 = (bf16[16,4096]{1,0:T(8,128)(2,1)}, bf16[16,4096]{1,0:T(8,128)(2,1)S(1)}, u32[]{:S(2)}) copy-start(bf16[16,4096]{1,0:T(8,128)(2,1)S(1)} %convert_element_type.7) | copy-start | bytes 393220
  128.3 102.4 %all-gather.11.cloned.1.call-start = ((), (), s32[]{:S(2)}) async-start(), calls=%async_computation.11 | async-start | bytes 8650752 | tf_op jit(solution)/shard_map/all_gather | solution.py:119
  128.4 0.7 collective-permute-start
  129.1 0.7 copy-start.8
  129.8 142.4 %all-reduce.4.cloned.1.call-start = ((), (), s32[]{:S(2)}) async-start(), calls=%async_computation.5 | async-start | bytes 524288 | tf_op jit(solution)/shard_map/psum | solution.py:151
  177.4 135.9 %reduce-scatter.6.cloned.1.call-start = ((), (), s32[]{:S(2)}) async-start(), calls=%async_computation.6 | async-start | bytes 1310720 | tf_op jit(solution)/shard_map/reduce_scatter | solution.py:161
  230.7 41.6 %copy-start.5 = (bf16[256,4096]{1,0:T(8,128)(2,1)S(1)}, bf16[256,4096]{1,0:T(8,128)(2,1)}, u32[]{:S(2)}) copy-start(bf16[256,4096]{1,0:T(8,128)(2,1)} %all-gather.7.cloned.1.call-done) | copy-start | bytes 6291460
  272.2 8.3 copy-start.4
  277.1 3.4 copy-start.2
  288.2 96.9 %all-gather.13.cloned.1.call-start = ((), (), s32[]{:S(2)}) async-start(), calls=%async_computation.12 | async-start | bytes 8650752 | tf_op jit(solution)/shard_map/all_gather | solution.py:119
  313.3 1.6 collective-permute-start.1
  314.9 0.7 copy-start.9
  315.6 222.4 %all-reduce.6.cloned.1.call-start = ((), (), s32[]{:S(2)}) async-start(), calls=%async_computation.7 | async-start | bytes 2097152 | tf_op jit(solution)/shard_map/psum | solution.py:165
  318.3 405.0 %reduce-scatter.8.cloned.1.call-start = ((), (), s32[]{:S(2)}) async-start(), calls=%async_computation.8 | async-start | bytes 1310720 | tf_op jit(solution)/shard_map/reduce_scatter | solution.py:161
  389.5 3.3 copy-start.3
  403.4 470.5 %all-reduce.8.cloned.1.call-start = ((), (), s32[]{:S(2)}) async-start(), calls=%async_computation.10 | async-start | bytes 2097152 | tf_op jit(solution)/shard_map/psum | solution.py:170
  725.2 1.7 copy-start.6
  726.9 169.1 %all-gather.9.cloned.1.call-start = ((), (), s32[]{:S(2)}) async-start(), calls=%async_computation.9 | async-start | bytes 1310720 | tf_op jit(solution)/shard_map/all_gather | solution.py:169
  873.9 25.6 %copy-start.1 = (f32[512,512]{1,0:T(8,128)S(1)}, f32[512,512]{1,0:T(8,128)}, u32[]{:S(2)}) copy-start(f32[512,512]{1,0:T(8,128)} %param.9) | copy-start | bytes 3145732
Sparse Core Ops, SparseCore 0:
  31.2 95.1 reduce-scatter.3
  129.2 46.3 all-gather.6
  178.5 52.1 all-gather.10
  233.4 38.7 all-reduce.3
  288.4 24.8 reduce-scatter.5
  316.0 69.0 all-gather.12
  390.5 147.4 all-reduce.5
  540.4 20.8 reduce-scatter.7
  727.0 146.8 all-reduce.7
  875.4 20.5 all-gather.8

commit v2 on v1

--- a/solution.py
+++ b/solution.py
@@ -104,27 +104,504 @@
     )
 
 
-def swap_axes(share, planes, group):
-    perm = [
-        ((z * group + r) * planes + t, (t * group + r) * planes + z)
-        for z in range(planes)
-        for r in range(group)
-        for t in range(planes)
+MESH = pl.DeviceIdType.MESH
+RING = 4
+
+
+class Place:
+    def __init__(self):
+        f = lax.axis_index("fsdp")
+        self.t = lax.axis_index("tensor")
+        self.c = lax.rem(f, 2)
+        self.x = lax.rem(lax.div(f, 2), RING)
+        self.z = lax.div(f, 2 * RING)
+
+    def along(self, axis, step):
+        return lax.rem(getattr(self, axis) + (step + RING), RING)
+
+    def device(self, **moved):
+        at = {name: moved.get(name, getattr(self, name)) for name in ("z", "x", "c", "t")}
+        return {"fsdp": (at["z"] * RING + at["x"]) * 2 + at["c"], "tensor": at["t"]}
+
+    def ahead(self, axis, step):
+        return self.device(**{axis: self.along(axis, step)})
+
+    def other_core(self):
+        return self.device(c=1 - self.c)
+
+
+def meet(devices, place=None):
+    barrier = pltpu.get_barrier_semaphore()
+    for device in devices:
+        pl.semaphore_signal(barrier, inc=1, device_id=device, device_id_type=MESH)
+    count = len(devices)
+    if place is not None:
+
+        @pl.when(place.t != place.z)
+        def _():
+            pl.semaphore_signal(
+                barrier, inc=1, device_id=place.device(z=place.t, t=place.z), device_id_type=MESH
+            )
+
+        count = count + jnp.where(place.t != place.z, 1, 0)
+    pl.semaphore_wait(barrier, count)
+
+
+class Links:
+    def __init__(self, send, recv):
+        self.send, self.recv, self.started = send, recv, []
+
+    def copy(self, src, dst, device):
+        i = len(self.started)
+        made = pltpu.make_async_remote_copy(
+            src_ref=src,
+            dst_ref=dst,
+            send_sem=self.send.at[i],
+            recv_sem=self.recv.at[i],
+            device_id=device,
+            device_id_type=MESH,
+        )
+        self.started.append(made)
+        return made
+
+    def go(self, src, dst, device):
+        made = self.copy(src, dst, device)
+        made.start()
+        return made
+
+
+def gather_plane(own, out, slot, width, links, place):
+    half, piece = width // 2, width // 4
+    ways = ((0, "x", "z"), (1, "z", "x"))
+
+    def at(z, x, cols):
+        return out.at[slot(z, x, place.c) + (slice(None), cols)]
+
+    def spot(axis, step, cols):
+        z = place.along("z", step) if axis == "z" else place.z
+        x = place.along("x", step) if axis == "x" else place.x
+        return at(z, x, cols)
+
+    def line(axis, other, step, cols):
+        if axis == "x":
+            return at(place.along(other, step), slice(None), cols)
+        return at(slice(None), place.along(other, step), cols)
+
+    def half_cols(h):
+        return pl.ds(h * half, half)
+
+    def piece_cols(h, d):
+        return pl.ds(h * half + (0 if d > 0 else piece), piece)
+
+    first, second, third, fourth, rest = {}, {}, {}, {}, []
+    for h, axis, _ in ways:
+        for d in (1, -1):
+            cols = half_cols(h)
+            first[h, d] = links.go(own.at[:, cols], spot(axis, 0, cols), place.ahead(axis, d))
+    for h, axis, _ in ways:
+        for d in (1, -1):
+            first[h, d].wait_recv()
+            cols = piece_cols(h, d)
+            chunk = spot(axis, -d, cols)
+            second[h, d] = links.go(chunk, chunk, place.ahead(axis, d))
+    return ways, line, half_cols, piece_cols, second, third, fourth, rest
+
+
+def finish_plane(parts, links, place):
+    ways, line, half_cols, piece_cols, second, third, fourth, rest = parts
+    for h, axis, other in ways:
+        for d in (1, -1):
+            second[h, d].wait_recv()
+        whole = line(axis, other, 0, half_cols(h))
+        for d in (1, -1):
+            third[h, d] = links.go(whole, whole, place.ahead(other, d))
+        rest.append(links.go(whole, whole, place.other_core()))
+    for h, axis, other in ways:
+        for d in (1, -1):
+            third[h, d].wait_recv()
+            part = line(axis, other, -d, piece_cols(h, d))
+            fourth[h, d] = links.go(part, part, place.ahead(other, d))
+            whole = line(axis, other, -d, half_cols(h))
+            rest.append(links.go(whole, whole, place.other_core()))
+    for h, axis, other in ways:
+        for d in (1, -1):
+            fourth[h, d].wait_recv()
+            part = line(axis, other, -2 * d, piece_cols(h, d))
+            rest.append(links.go(part, part, place.other_core()))
+    for made in rest:
+        made.wait_recv()
+
+
+GATHER_COPIES = 26
+
+
+def plane_neighbours(place):
+    return [place.ahead(axis, d) for axis in ("x", "z") for d in (1, -1)] + [place.other_core()]
+
+
+def by_column(z, x, c):
+    return (x, c, z)
+
+
+def by_token(z, x, c):
+    return (z, x, c)
+
+
+def swap_in(share, out, links, place, sem):
+    sent = links.copy(
+        share, out.at[by_column(place.t, place.x, place.c)], place.device(z=place.t, t=place.z)
+    )
+
+    @pl.when(place.t != place.z)
+    def _():
+        sent.start()
+        sent.wait_recv()
+
+    @pl.when(place.t == place.z)
+    def _():
+        kept = pltpu.make_async_copy(share, out.at[by_column(place.z, place.x, place.c)], sem)
+        kept.start()
+        kept.wait()
+
+    return sent
+
+
+def settle(links, place, swapped):
+    for made in links.started:
+        if made is swapped:
+
+            @pl.when(place.t != place.z)
+            def _():
+                made.wait_send()
+        else:
+            made.wait_send()
+
+
+def spread_kernel(share_ref, out_ref, send, recv, sem):
+    place = Place()
+    links = Links(send, recv)
+    meet(plane_neighbours(place), place)
+    swapped = swap_in(share_ref, out_ref, links, place, sem)
+    own = out_ref.at[by_column(place.z, place.x, place.c)]
+    parts = gather_plane(own, out_ref, by_column, share_ref.shape[1], links, place)
+    finish_plane(parts, links, place)
+    settle(links, place, swapped)
+
+
+def spread(share, collective_id):
+    rows, width = share.shape
+    out = pl.pallas_call(
+        spread_kernel,
+        out_shape=jax.ShapeDtypeStruct((RING, 2, RING, rows, width), share.dtype),
+        in_specs=[pl.BlockSpec(memory_space=pltpu.VMEM)],
+        out_specs=pl.BlockSpec(memory_space=pl.ANY),
+        scratch_shapes=[
+            pltpu.SemaphoreType.DMA((GATHER_COPIES + 1,)),
+            pltpu.SemaphoreType.DMA((GATHER_COPIES + 1,)),
+            pltpu.SemaphoreType.DMA,
+        ],
+        compiler_params=pltpu.CompilerParams(collective_id=collective_id, has_side_effects=True),
+        name="spread",
+    )(share)
+    return out.reshape(-1, width)
+
+
+def reduce_y(part_ref, share_ref, relay, build, arrive, links, place):
+    rows, width = share_ref.shape
+    half = width // 2
+    low, high = pl.ds(0, half), pl.ds(half, half)
+
+    def quarter(step, cols):
+        start = pl.multiple_of(place.along("t", step) * rows, rows)
+        return part_ref.at[pl.ds(start, rows), cols]
+
+    up, down = place.ahead("t", 1), place.ahead("t", -1)
+    far_up = links.go(quarter(2, low), relay.at[0], up)
+    far_down = links.go(quarter(2, high), relay.at[1], down)
+    near_up = links.go(quarter(1, high), arrive.at[0, :, high], up)
+    near_down = links.go(quarter(-1, low), arrive.at[1, :, low], down)
+    far_up.wait_recv()
+    build[0] = quarter(1, low)[...] + relay[0]
+    sum_up = links.go(build.at[0], arrive.at[0, :, low], up)
+    far_down.wait_recv()
+    build[1] = quarter(-1, high)[...] + relay[1]
+    sum_down = links.go(build.at[1], arrive.at[1, :, high], down)
+    for made in (near_up, near_down, sum_up, sum_down):
+        made.wait_recv()
+    share_ref[...] = quarter(0, pl.ds(0, width))[...] + (arrive[0] + arrive[1])
+
+
+REDUCE_COPIES = 6
+
+
+def reduce_scratch(rows, width):
+    return [
+        pltpu.VMEM((2, rows, width // 2), F32),
+        pltpu.VMEM((2, rows, width // 2), F32),
+        pltpu.VMEM((2, rows, width), F32),
     ]
-    return lax.ppermute(share, ("fsdp", "tensor"), perm)
-
-
-def spread(share, planes, group):
-    moved = swap_axes(share, planes, group)
-    whole = lax.all_gather(moved, "fsdp", axis=0)
-    rows, width = share.shape
-    return whole.reshape(planes, group, rows, width).transpose(1, 0, 2, 3).reshape(-1, width)
+
+
+def y_neighbours(place):
+    return [place.ahead("t", 1), place.ahead("t", -1)]
+
+
+def reduce_kernel(part_ref, share_ref, relay, build, arrive, send, recv):
+    place = Place()
+    links = Links(send, recv)
+    meet(y_neighbours(place))
+    reduce_y(part_ref, share_ref, relay, build, arrive, links, place)
+    for made in links.started:
+        made.wait_send()
+
+
+def reduce_over_y(part, collective_id):
+    rows, width = part.shape[0] // RING, part.shape[1]
+    return pl.pallas_call(
+        reduce_kernel,
+        out_shape=jax.ShapeDtypeStruct((rows, width), F32),
+        in_specs=[pl.BlockSpec(memory_space=pltpu.VMEM)],
+        out_specs=pl.BlockSpec(memory_space=pltpu.VMEM),
+        scratch_shapes=reduce_scratch(rows, width)
+        + [pltpu.SemaphoreType.DMA((REDUCE_COPIES,)), pltpu.SemaphoreType.DMA((REDUCE_COPIES,))],
+        compiler_params=pltpu.CompilerParams(collective_id=collective_id, has_side_effects=True),
+        name="reduce_over_y",
+    )(part)
+
+
+def reduce_spread_kernel(part_ref, share_ref, out_ref, relay, build, arrive, send, recv, sem):
+    place = Place()
+    links = Links(send, recv)
+    meet(plane_neighbours(place) + y_neighbours(place), place)
+    reduce_y(part_ref, share_ref, relay, build, arrive, links, place)
+    swapped = swap_in(share_ref, out_ref, links, place, sem)
+    own = out_ref.at[by_column(place.z, place.x, place.c)]
+    parts = gather_plane(own, out_ref, by_column, share_ref.shape[1], links, place)
+    finish_plane(parts, links, place)
+    settle(links, place, swapped)
+
+
+def reduce_and_spread(part, collective_id):
+    rows, width = part.shape[0] // RING, part.shape[1]
+    copies = REDUCE_COPIES + 1 + GATHER_COPIES
+    share, out = pl.pallas_call(
+        reduce_spread_kernel,
+        out_shape=(
+            jax.ShapeDtypeStruct((rows, width), F32),
+            jax.ShapeDtypeStruct((RING, 2, RING, rows, width), F32),
+        ),
+        in_specs=[pl.BlockSpec(memory_space=pltpu.VMEM)],
+        out_specs=(pl.BlockSpec(memory_space=pltpu.VMEM), pl.BlockSpec(memory_space=pl.ANY)),
+        scratch_shapes=reduce_scratch(rows, width)
+        + [
+            pltpu.SemaphoreType.DMA((copies,)),
+            pltpu.SemaphoreType.DMA((copies,)),
+            pltpu.SemaphoreType.DMA,
+        ],
+        compiler_params=pltpu.CompilerParams(collective_id=collective_id, has_side_effects=True),
+        name="reduce_and_spread",
+    )(part)
+    return share, out.reshape(-1, width)
+
+
+def kept_kernel(kept_ref, rows_ref, cols_ref, send, recv, sem):
+    place = Place()
+    links = Links(send, recv)
+    meet(plane_neighbours(place) + y_neighbours(place))
+    local = pltpu.make_async_copy(kept_ref, rows_ref.at[by_token(place.z, place.x, place.c)], sem)
+    local.start()
+    parts = gather_plane(kept_ref, rows_ref, by_token, kept_ref.shape[1], links, place)
+    local.wait()
+    finish_plane(parts, links, place)
+    for made in links.started:
+        made.wait_send()
+    width = cols_ref.shape[-1]
+    start = pl.multiple_of((place.x * 2 + place.c) * width, width)
+    source = rows_ref.at[:, :, :, :, pl.ds(start, width)]
+    distance = lax.rem(place.t - place.z + RING, RING)
+    up, down = place.ahead("t", 1), place.ahead("t", -1)
+    to_up = links.copy(source, cols_ref, up)
+    to_down = links.copy(source, cols_ref, down)
+    low = cols_ref.at[pl.ds(0, RING // 2)]
+    high = cols_ref.at[pl.ds(RING // 2, RING // 2)]
+    on_up = links.copy(low, low, up)
+    on_down = links.copy(high, high, down)
+
+    @pl.when(distance == 0)
+    def _():
+        to_up.start()
+        to_down.start()
+        own = pltpu.make_async_copy(source, cols_ref, sem)
+        own.start()
+        own.wait()
+        to_up.wait_send()
+        to_down.wait_send()
+
+    @pl.when(distance == 1)
+    def _():
+        to_up.wait_recv()
+        on_up.start()
+        on_up.wait_send()
+
+    @pl.when(distance == 3)
+    def _():
+        to_down.wait_recv()
+        on_down.start()
+        on_down.wait_send()
+
+    @pl.when(distance == 2)
+    def _():
+        on_up.wait_recv()
+        on_down.wait_recv()
+
+
+def gather_kept(kept, tile_width, collective_id):
+    rows, width = kept.shape
+    lead = (RING, RING, 2, rows)
+    copies = GATHER_COPIES + 4
+    kept_rows, kept_cols = pl.pallas_call(
+        kept_kernel,
+        out_shape=(
+            jax.ShapeDtypeStruct(lead + (width,), kept.dtype),
+            jax.ShapeDtypeStruct(lead + (tile_width,), kept.dtype),
+        ),
+        in_specs=[pl.BlockSpec(memory_space=pltpu.VMEM)],
+        out_specs=(pl.BlockSpec(memory_space=pltpu.VMEM), pl.BlockSpec(memory_space=pltpu.VMEM)),
+        scratch_shapes=[
+            pltpu.SemaphoreType.DMA((copies,)),
+            pltpu.SemaphoreType.DMA((copies,)),
+            pltpu.SemaphoreType.DMA,
+        ],
+        compiler_params=pltpu.CompilerParams(collective_id=collective_id, has_side_effects=True),
+        name="gather_kept",
+    )(kept)
+    return kept_rows.reshape(-1, width), kept_cols.reshape(-1, tile_width)
+
+
+def total_kernel(with_rows, *refs):
+    if with_rows:
+        gram_ref, rows_ref, out_ref, all_ref = refs[:4]
+        refs = refs[4:]
+    else:
+        gram_ref, out_ref = refs[:2]
+        refs = refs[2:]
+    pair, mine, first, second, last, sum_one, sum_two, send, recv = refs
+    place = Place()
+    links = Links(send, recv)
+    n = gram_ref.shape[0]
+    half, width = n // 2, n // 2
+    block, piece = half // RING, half // RING // RING
+    ways = (("x", "z", pl.ds(0, width)), ("z", "x", pl.ds(width, width)))
+    meet(
+        [place.other_core()]
+        + [place.ahead(axis, k) for axis in ("x", "z", "t") for k in (1, 2, 3)]
+    )
+    kept_base = pl.multiple_of(place.c * half, half)
+    gone_base = pl.multiple_of((1 - place.c) * half, half)
+    swapped = links.go(gram_ref.at[pl.ds(gone_base, half)], pair, place.other_core())
+    relayed = []
+    if with_rows:
+        around = all_ref.at[place.t]
+        relayed = [links.go(rows_ref, around, place.ahead("t", d)) for d in (1, -1)]
+        all_ref[pl.ds(place.t, 1)] = rows_ref[...][None]
+    swapped.wait_recv()
+    mine[...] = gram_ref[pl.ds(kept_base, half), :] + pair[...]
+    sent = {}
+    for p, (axis, other, cols) in enumerate(ways):
+        for k in (1, 2, 3):
+            start = pl.multiple_of(place.along(axis, k) * block, block)
+            sent[p, k] = links.go(
+                mine.at[pl.ds(start, block), cols], first.at[p, k - 1], place.ahead(axis, k)
+            )
+    for p, (axis, other, cols) in enumerate(ways):
+        for k in (1, 2, 3):
+            sent[p, k].wait_recv()
+        start = pl.multiple_of(getattr(place, axis) * block, block)
+        sum_one[p] = (mine[pl.ds(start, block), cols] + first[p, 0]) + (first[p, 1] + first[p, 2])
+        for k in (1, 2, 3):
+            start = pl.multiple_of(place.along(other, k) * piece, piece)
+            sent[p, k] = links.go(
+                sum_one.at[p, pl.ds(start, piece)], second.at[p, k - 1], place.ahead(other, k)
+            )
+    for p, (axis, other, cols) in enumerate(ways):
+        for k in (1, 2, 3):
+            sent[p, k].wait_recv()
+        start = pl.multiple_of(getattr(place, other) * piece, piece)
+        sum_two[p] = (sum_one[p, pl.ds(start, piece), :] + second[p, 0]) + (second[p, 1] + second[p, 2])
+        for k in (1, 2, 3):
+            sent[p, k] = links.go(sum_two.at[p], last.at[p, place.t], place.ahead("t", k))
+        last[p, pl.ds(place.t, 1)] = sum_two[p][None]
+    for p, (axis, other, cols) in enumerate(ways):
+        for k in (1, 2, 3):
+            sent[p, k].wait_recv()
+        base = kept_base + getattr(place, axis) * block
+        start = pl.multiple_of(base + getattr(place, other) * piece, piece)
+        final = out_ref.at[pl.ds(start, piece), cols]
+        final[...] = (last[p, 0] + last[p, 1]) + (last[p, 2] + last[p, 3])
+        for k in (1, 2, 3):
+            sent[p, k] = links.go(final, final, place.ahead(other, k))
+    if with_rows:
+        part = rows_ref.shape[0] // 2
+        onward = []
+        for d, made in zip((1, -1), relayed):
+            made.wait_recv()
+            held = all_ref.at[place.along("t", -d), pl.ds(0 if d > 0 else part, part)]
+            onward.append(links.go(held, held, place.ahead("t", d)))
+    for p, (axis, other, cols) in enumerate(ways):
+        for k in (1, 2, 3):
+            sent[p, k].wait_recv()
+        start = pl.multiple_of(kept_base + getattr(place, axis) * block, block)
+        whole = out_ref.at[pl.ds(start, block), cols]
+        for k in (1, 2, 3):
+            sent[p, k] = links.go(whole, whole, place.ahead(axis, k))
+    for p in range(2):
+        for k in (1, 2, 3):
+            sent[p, k].wait_recv()
+    side = out_ref.at[pl.ds(kept_base, half)]
+    links.go(side, side, place.other_core()).wait_recv()
+    if with_rows:
+        for made in onward:
+            made.wait_recv()
+    for made in links.started:
+        made.wait_send()
+
+
+def total_gram(gram, collective_id, rows=None):
+    n = gram.shape[0]
+    block, piece = n // 2 // RING, n // 2 // RING // RING
+    copies = 2 + 30 + (4 if rows is not None else 0)
+    shapes = [jax.ShapeDtypeStruct((n, n), F32)]
+    operands = [gram]
+    if rows is not None:
+        shapes.append(jax.ShapeDtypeStruct((RING,) + rows.shape, F32))
+        operands.append(rows)
+    vmem = pl.BlockSpec(memory_space=pltpu.VMEM)
+    out = pl.pallas_call(
+        functools.partial(total_kernel, rows is not None),
+        out_shape=tuple(shapes),
+        in_specs=[vmem] * len(operands),
+        out_specs=tuple([vmem] * len(shapes)),
+        scratch_shapes=[
+            pltpu.VMEM((n // 2, n), F32),
+            pltpu.VMEM((n // 2, n), F32),
+            pltpu.VMEM((2, 3, block, n // 2), F32),
+            pltpu.VMEM((2, 3, piece, n // 2), F32),
+            pltpu.VMEM((2, RING, piece, n // 2), F32),
+            pltpu.VMEM((2, block, n // 2), F32),
+            pltpu.VMEM((2, piece, n // 2), F32),
+            pltpu.SemaphoreType.DMA((copies,)),
+            pltpu.SemaphoreType.DMA((copies,)),
+        ],
+        compiler_params=pltpu.CompilerParams(collective_id=collective_id, has_side_effects=True),
+        name="total_gram",
+    )(*operands)
+    if rows is None:
+        return out[0]
+    return out[0], out[1].reshape(-1, rows.shape[1])
 
 
 def body(hidden, down_weight, covariance, keep_index, start_basis):
     fsdp_count = lax.axis_size("fsdp")
-    planes = lax.axis_size("tensor")
-    group = fsdp_count // planes
     total_tokens = TOK_DEV * fsdp_count
     quarter, block_width = covariance.shape
     share_rows = quarter // fsdp_count
@@ -133,7 +610,7 @@
     root = math.sqrt(D)
 
     start_share = lax.dynamic_slice_in_dim(start_basis, t * share_rows, share_rows, 0)
-    start_rows = spread(start_share, planes, group)
+    start_rows = spread(start_share, 1)
 
     all_hidden = lax.all_gather(hidden, "tensor", axis=0, tiled=True)
     mlp_out = lax.psum_scatter(
@@ -146,29 +623,24 @@
     positions = jnp.arange(mlp_out.shape[0], dtype=jnp.int32)
     chosen = (listed[:, None] == positions[None, :]).astype(BF16)
     kept = jnp.dot(chosen, mlp_out, preferred_element_type=F32).astype(BF16)
-    kept_rows = lax.all_gather(kept, "fsdp", axis=0, tiled=True)
-    own = lax.dynamic_slice_in_dim(kept_rows, f % group * block_width, block_width, 1)
-    kept_cols = lax.psum(jnp.where(t == f // group, own, jnp.zeros_like(own)), "tensor")
+    kept_rows, kept_cols = gather_kept(kept, block_width, 2)
     update = lax.dot_general(
         kept_rows, kept_cols, (((0,), (0,)), ((), ())), preferred_element_type=F32
     )
     new_covariance = covariance + update * (1.0 / total_tokens)
 
-    def image_share(rows):
-        partial = lax.dot_general(
+    def image_part(rows):
+        return lax.dot_general(
             new_covariance, rows, (((0,), (0,)), ((), ())), precision=HIGH, preferred_element_type=F32
         )
-        return lax.psum_scatter(partial, "tensor", scatter_dimension=0, tiled=True)
-
-    image_one = image_share(start_rows)
-    image_rows = spread(image_one, planes, group)
-    inverse_one = inverse_factor(lax.psum(gram_of(image_one), ("fsdp", "tensor")))
+
+    image_one, image_rows = reduce_and_spread(image_part(start_rows), 3)
+    inverse_one = inverse_factor(total_gram(gram_of(image_one), 4))
     own_rows = lax.dynamic_slice_in_dim(image_rows, f * share_rows, share_rows, 0)
     first_basis = times_transpose(own_rows, inverse_one, root)
-    image_two = times_transpose(image_share(image_rows), inverse_one)
-    whole_two = lax.all_gather(image_two, "tensor", axis=0, tiled=True)
-    inverse_two = inverse_factor(lax.psum(gram_of(image_two), ("fsdp", "tensor")))
-    final_basis = times_transpose(whole_two, inverse_two, root)
+    image_two = times_transpose(reduce_over_y(image_part(image_rows), 5), inverse_one)
+    total_two, whole_two = total_gram(gram_of(image_two), 6, image_two)
+    final_basis = times_transpose(whole_two, inverse_factor(total_two), root)
     return (mlp_out, new_covariance, first_basis, final_basis)
 
 

time: 908 us -> 551 us (0.61)
  waiting for transfers between devices: 609 us -> 39.8 us
  Pallas kernels: 196 us -> 423 us
  local copies, waits for them, and re-layouts: 20.9 us -> 4.15 us
    psum x3 -> x0, waiting for transfers between devices: 311 us -> none  [the longest x1 144 us: body(): lax.psum(gram_of(image_two), ('fsdp', 'tensor'))]
    pallas_call x0 -> x6, Pallas kernels: none -> 227 us  [the longest x1 67.8 us: reduce_and_spread(): pl.pallas_call(reduce_spread_kernel, out_shape=(jax.ShapeDtypeStruct((row...]
    all_gather x4 -> x0, waiting for transfers between devices: 176 us -> none  [the longest x2 120 us: spread(): whole = lax.all_gather(moved, 'fsdp', axis=0)]
    reduce_scatter x1, waiting for transfers between devices: 95.2 us -> 39.8 us  [body(): lax.psum_scatter(jnp.dot(all_hidden, down_weight, preferred_element_type=...]
    reduce_scatter x2 -> x0, waiting for transfers between devices: 25 us -> none  [image_share(): return lax.psum_scatter(partial, 'tensor', scatter_dimension=0, tiled=True)]
  transfers between devices with their start and end apart: 12 -> 1, of which waited for: 9 -> 1; matrix products, arithmetic and copies ran while one was open for 3% -> 0% of each run, Pallas kernels for 22% -> 10%
where the time goes in v2:
time: 551 us
  Pallas kernels  423 us (77%)
  matrix products  54.3 us (10%)
  waiting for transfers between devices  39.8 us (7%)
  between operations  14.2 us (3%)
  blocking collectives  14.1 us (3%)
    pallas_call x2, Pallas kernels, inverse_factor(): pl.pallas_call(inverse_factor_kernel, out_shape=jax.ShapeDtypeStruct((n,...  197 us
    pallas_call x1, Pallas kernels, reduce_and_spread(): pl.pallas_call(reduce_spread_kernel, out_shape=(jax.ShapeDtypeStruct((row...  67.8 us
    pallas_call x2, Pallas kernels, total_gram(): pl.pallas_call(functools.partial(total_kernel, rows is not None), out_sha...  59.8 us
    pallas_call x1, Pallas kernels, spread(): pl.pallas_call(spread_kernel, out_shape=jax.ShapeDtypeStruct((RING, 2, RI...  54.8 us
    reduce_scatter x1, waiting for transfers between devices, body(): lax.psum_scatter(jnp.dot(all_hidden, down_weight, preferred_element_type=...  39.8 us
    pallas_call x1, Pallas kernels, gather_kept(): pl.pallas_call(kept_kernel, out_shape=(jax.ShapeDtypeStruct(lead + (width...  30.3 us
    dot_general x2, matrix products, image_part(): lax.dot_general(new_covariance, rows, (((0,), (0,)), ((), ())), precision...  26.8 us
    all_gather x1, blocking collectives, body(): all_hidden = lax.all_gather(hidden, 'tensor', axis=0, tiled=True)  14.1 us
  transfers between devices with their start and end apart: 1, of which 1 were waited for; matrix products, arithmetic and copies ran while one was open for 0% of the time, Pallas kernels for 10%

profile of v2, /device:TPU:1, one launch (start us, length us, event | category | flops | bytes accessed | tf_op | source)
XLA Modules:
  0.0 550.7 jit_solution(14357608764161261465)
XLA Ops:
  7.2 0.0 reduce-scatter.2.cloned.1.call-start
  7.2 14.1 %all_gather.3 = bf16[512,896]{1,0:T(8,128)(2,1)S(1)} all-gather(bf16[128,896]{1,0:T(8,128)(2,1)} %param.5), channel_id=1, replica_groups=mesh['fsdp'=32,'tensor'=4] {'tensor'}, dimensions={0}, use_global_device_ids=true | all-gather | bytes 1146880 | tf_op jit(solution)/shard_map/all_gather | solution.py:615
  21.3 9.8 %fusion.4 = f32[512,4096]{1,0:T(8,128)} fusion(bf16[512,896]{1,0:T(8,128)(2,1)S(1)} %all_gather.3, bf16[896,4096]{1,0:T(8,128)(2,1)} %param.6), kind=kOutput, calls=%fused_computation.10 | convolution fusion | flops 3758096384 | bytes 16646144 | tf_op jit(solution)/shard_map/dot_general | solution.py:617
  31.1 0.7 constant_dynamic-slice_fusion.share_ref
  31.9 54.8 %spread.1 = f32[4,2,4,128,512]{4,3,2,1,0:T(8,128)} custom-call(f32[128,512]{1,0:T(8,128)} %constant_dynamic-slice_fusion.share_ref), custom_call_target="tpu_custom_call" | custom-call | tf_op jit(solution)/shard_map/spread/pallas_call | solution.py:293
  86.6 39.8 %reduce-scatter.2.cloned.1.call-done = f32[16,4096]{1,0:T(8,128)} async-done(((f32[512,4096]{1,0:T(8,128)}), f32[16,4096]{1,0:T(8,128)}) %reduce-scatter.2.cloned.1.call-update) | async-done | bytes 262160 | tf_op jit(solution)/shard_map/reduce_scatter | solution.py:616
  126.4 1.0 convert_element_type.7
  127.4 0.8 convolution_convert_fusion.kept_ref
  128.2 30.3 %gather_kept.1 = (bf16[4,4,2,8,4096]{4,3,2,1,0:T(8,128)(2,1)}, bf16[4,4,2,8,512]{4,3,2,1,0:T(8,128)(2,1)}) custom-call(bf16[8,4096]{1,0:T(8,128)(2,1)} %convolution_convert_fusion.kept_ref), custom_call_target="tpu_custom_call" | custom-call | tf_op jit(solution)/shard_map/gather_kept/pallas_call | solution.py:462
  158.6 5.5 %fusion = f32[4096,512]{1,0:T(8,128)S(1)} fusion(f32[4096,512]{1,0:T(8,128)} %param.7, bf16[4,4,2,8,4096]{4,3,2,1,0:T(8,128)(2,1)} %get-tuple-element.10, bf16[4,4,2,8,512]{4,3,2,1,0:T(8,128)(2,1)} %get-tuple-element.11), kind=kOutput, calls=%fused_computation.1 | convolution fusion | flops 1077936128 | bytes 19136512 | tf_op jit(solution)/shard_map/dot_general | solution.py:627
  164.1 3.4 copy-done.1
  167.5 7.7 %fusion.5.part_ref = f32[512,512]{1,0:T(8,128)} fusion(f32[4096,512]{1,0:T(8,128)S(1)} %fusion, f32[4096,512]{1,0:T(8,128)S(1)} %bitcast.28), kind=kOutput, calls=%fused_computation.11 | convolution fusion | flops 6442450944 | bytes 17825792 | tf_op jit(solution)/shard_map/dot_general | solution.py:633
  175.2 67.8 %reduce_and_spread.1 = (f32[128,512]{1,0:T(8,128)}, f32[4,2,4,128,512]{4,3,2,1,0:T(8,128)}) custom-call(f32[512,512]{1,0:T(8,128)} %fusion.5.part_ref), custom_call_target="tpu_custom_call" | custom-call | tf_op jit(solution)/shard_map/reduce_and_spread/pallas_call | solution.py:387
  243.0 2.6 fusion.6.refs_0_
  245.6 30.0 %total_gram.2.gram_ref = f32[512,512]{1,0:T(8,128)} custom-call(f32[512,512]{1,0:T(8,128)} %fusion.6.refs_0_), custom_call_target="tpu_custom_call" | custom-call | tf_op jit(solution)/shard_map/total_gram/pallas_call | solution.py:579
  275.6 185.5 %inverse_factor.2 = f32[512,512]{1,0:T(8,128)} custom-call(f32[512,512]{1,0:T(8,128)} %total_gram.2.gram_ref), custom_call_target="tpu_custom_call" | custom-call | flops 8000000000 | bytes 2097152 | tf_op jit(solution)/shard_map/inverse_factor/pallas_call | solution.py:83
  461.1 19.1 %fusion.7.part_ref = f32[512,512]{1,0:T(8,128)} fusion(f32[4096,512]{1,0:T(8,128)} %copy-done.1, f32[4096,512]{1,0:T(8,128)} %bitcast.29), kind=kOutput, calls=%fused_computation.13 | convolution fusion | flops 6442450944 | bytes 17825792 | tf_op jit(solution)/shard_map/dot_general | solution.py:633
  480.2 13.9 %reduce_over_y.1 = f32[128,512]{1,0:T(8,128)} custom-call(f32[512,512]{1,0:T(8,128)} %fusion.7.part_ref), custom_call_target="tpu_custom_call" | custom-call | tf_op jit(solution)/shard_map/reduce_over_y/pallas_call | solution.py:360
  494.1 2.3 convolution_multiply_fusion.1
  496.4 1.6 fusion.8.refs_1_
  498.0 1.6 fusion.9.refs_0_
  499.6 29.9 %total_gram.3 = (f32[512,512]{1,0:T(8,128)}, f32[4,128,512]{2,1,0:T(8,128)}) custom-call(f32[512,512]{1,0:T(8,128)} %fusion.9.refs_0_, f32[128,512]{1,0:T(8,128)} %copy-done.3), custom_call_target="tpu_custom_call" | custom-call | tf_op jit(solution)/shard_map/total_gram/pallas_call | solution.py:579
  529.5 11.1 %inverse_factor.3 = f32[512,512]{1,0:T(8,128)} custom-call(f32[512,512]{1,0:T(8,128)} %get-tuple-element.15.gram_ref), custom_call_target="tpu_custom_call" | custom-call | flops 8000000000 | bytes 2097152 | tf_op jit(solution)/shard_map/inverse_factor/pallas_call | solution.py:83
  540.6 3.2 convolution_multiply_fusion
  (16 shorter events, 0.1 us)
Async XLA Ops:
  7.2 24.0 %copy-start = (f32[512,512]{1,0:T(8,128)S(1)}, f32[512,512]{1,0:T(8,128)}, u32[]{:S(2)}) copy-start(f32[512,512]{1,0:T(8,128)} %param.9) | copy-start | bytes 3145732
  7.2 119.2 %reduce-scatter.2.cloned.1.call-start = ((), (), s32[]{:S(2)}) async-start(), calls=%async_computation.1 | async-start | bytes 8650752 | tf_op jit(solution)/shard_map/reduce_scatter | solution.py:616
  31.1 96.3 %copy-start.7 = (s32[1,8]{1,0:T(1,128)S(1)}, s32[1,8]{1,0:T(1,128)}, u32[]{:S(2)}) copy-start(s32[1,8]{1,0:T(1,128)} %param.8) | copy-start | bytes 100
  127.4 36.7 %copy-start.6 = (bf16[16,4096]{1,0:T(8,128)(2,1)}, bf16[16,4096]{1,0:T(8,128)(2,1)S(1)}, u32[]{:S(2)}) copy-start(bf16[16,4096]{1,0:T(8,128)(2,1)S(1)} %convert_element_type.7) | copy-start | bytes 393220
  158.5 9.0 %copy-start.2 = (f32[4,2,4,128,512]{4,3,2,1,0:T(8,128)S(1)}, f32[4,2,4,128,512]{4,3,2,1,0:T(8,128)}, u32[]{:S(2)}) copy-start(f32[4,2,4,128,512]{4,3,2,1,0:T(8,128)} %spread.1) | copy-start | bytes 25165828
  164.1 3.4 copy-start.1
  461.1 33.0 %copy-start.4 = (f32[512,512]{1,0:T(8,128)S(1)}, f32[512,512]{1,0:T(8,128)}, u32[]{:S(2)}) copy-start(f32[512,512]{1,0:T(8,128)} %inverse_factor.2) | copy-start | bytes 3145732
  498.0 1.6 copy-start.3
  529.5 11.1 %copy-start.5 = (f32[4,128,512]{2,1,0:T(8,128)S(1)}, f32[4,128,512]{2,1,0:T(8,128)}, u32[]{:S(2)}) copy-start(f32[4,128,512]{2,1,0:T(8,128)} %get-tuple-element.14) | copy-start | bytes 3145732
Sparse Core Ops, SparseCore 0:
  31.2 95.1 reduce-scatter.1

commit v3 on v2

--- a/solution.py
+++ b/solution.py
@@ -38,7 +38,7 @@
     eye = jnp.where(rows == cols, 1.0, 0.0)
     work[...] = eye - half_lower(scaled[...] - eye)
 
-    @pl.loop(0, 3)
+    @pl.loop(0, 2)
     def _(step):
         x = work[...]
         residual = residual_of(x, None)
@@ -48,18 +48,18 @@
 
     def unfinished(step):
         error = state[0]
-        return jnp.logical_and(step < 12, jnp.logical_not(error < 1e-5))
+        return jnp.logical_and(step < 12, jnp.logical_not(error < 1e-3))
 
     def refine(step):
         x = work[...]
         residual = residual_of(x, HIGH)
-        work[...] = x - jnp.dot(half_lower(residual), x, precision=HIGH, preferred_element_type=F32)
+        work[...] = x - jnp.dot(half_lower(residual), x, preferred_element_type=F32)
         state[0] = jnp.sum(residual * residual)
         return step + 1
 
     lax.while_loop(unfinished, refine, 0)
 
-    @pl.when(jnp.logical_not(state[0] < 1e-5))
+    @pl.when(jnp.logical_not(state[0] < 1e-3))
     def _():
         work[...] = eye
 
@@ -277,25 +277,55 @@
             made.wait_send()
 
 
-def spread_kernel(share_ref, out_ref, send, recv, sem):
+CODE_PAD = 16
+
+
+def encode(share, codes):
+    rows = share.shape[0]
+    largest = jnp.maximum(jnp.max(jnp.abs(share), axis=0, keepdims=True), 1e-30)
+    exponent = jnp.ceil(jnp.log2(largest) - 14.99)
+    scaled = jnp.clip(jnp.round(share * jnp.exp2(-exponent)), -32767.0, 32767.0)
+    codes[pl.ds(0, rows), :] = scaled.astype(jnp.int32).astype(jnp.int16)
+    marks = jnp.broadcast_to(exponent.astype(jnp.int32), (CODE_PAD, share.shape[1]))
+    codes[pl.ds(rows, CODE_PAD), :] = marks.astype(jnp.int16)
+    return scaled * jnp.exp2(exponent)
+
+
+def decode(codes):
+    wide = codes.astype(jnp.int32).astype(F32)
+    rows = codes.shape[0] - CODE_PAD
+    return wide[:rows] * jnp.exp2(wide[rows : rows + 1])
+
+
+def spread_codes(codes, out_ref, links, place, sem):
+    swapped = swap_in(codes, out_ref, links, place, sem)
+    own = out_ref.at[by_column(place.z, place.x, place.c)]
+    parts = gather_plane(own, out_ref, by_column, codes.shape[1], links, place)
+    finish_plane(parts, links, place)
+    settle(links, place, swapped)
+
+
+def spread_kernel(share_ref, out_ref, codes, send, recv, sem):
     place = Place()
     links = Links(send, recv)
     meet(plane_neighbours(place), place)
-    swapped = swap_in(share_ref, out_ref, links, place, sem)
-    own = out_ref.at[by_column(place.z, place.x, place.c)]
-    parts = gather_plane(own, out_ref, by_column, share_ref.shape[1], links, place)
-    finish_plane(parts, links, place)
-    settle(links, place, swapped)
+    encode(share_ref[...], codes)
+    spread_codes(codes, out_ref, links, place, sem)
+
+
+def spread_shape(rows, width):
+    return jax.ShapeDtypeStruct((RING, 2, RING, rows + CODE_PAD, width), jnp.int16)
 
 
 def spread(share, collective_id):
     rows, width = share.shape
-    out = pl.pallas_call(
+    return pl.pallas_call(
         spread_kernel,
-        out_shape=jax.ShapeDtypeStruct((RING, 2, RING, rows, width), share.dtype),
+        out_shape=spread_shape(rows, width),
         in_specs=[pl.BlockSpec(memory_space=pltpu.VMEM)],
         out_specs=pl.BlockSpec(memory_space=pl.ANY),
         scratch_shapes=[
+            pltpu.VMEM((rows + CODE_PAD, width), jnp.int16),
             pltpu.SemaphoreType.DMA((GATHER_COPIES + 1,)),
             pltpu.SemaphoreType.DMA((GATHER_COPIES + 1,)),
             pltpu.SemaphoreType.DMA,
@@ -303,7 +333,6 @@
         compiler_params=pltpu.CompilerParams(collective_id=collective_id, has_side_effects=True),
         name="spread",
     )(share)
-    return out.reshape(-1, width)
 
 
 def reduce_y(part_ref, share_ref, relay, build, arrive, links, place):
@@ -369,31 +398,26 @@
     )(part)
 
 
-def reduce_spread_kernel(part_ref, share_ref, out_ref, relay, build, arrive, send, recv, sem):
+def reduce_spread_kernel(part_ref, share_ref, out_ref, relay, build, arrive, codes, send, recv, sem):
     place = Place()
     links = Links(send, recv)
     meet(plane_neighbours(place) + y_neighbours(place), place)
     reduce_y(part_ref, share_ref, relay, build, arrive, links, place)
-    swapped = swap_in(share_ref, out_ref, links, place, sem)
-    own = out_ref.at[by_column(place.z, place.x, place.c)]
-    parts = gather_plane(own, out_ref, by_column, share_ref.shape[1], links, place)
-    finish_plane(parts, links, place)
-    settle(links, place, swapped)
+    share_ref[...] = encode(share_ref[...], codes)
+    spread_codes(codes, out_ref, links, place, sem)
 
 
 def reduce_and_spread(part, collective_id):
     rows, width = part.shape[0] // RING, part.shape[1]
     copies = REDUCE_COPIES + 1 + GATHER_COPIES
-    share, out = pl.pallas_call(
+    return pl.pallas_call(
         reduce_spread_kernel,
-        out_shape=(
-            jax.ShapeDtypeStruct((rows, width), F32),
-            jax.ShapeDtypeStruct((RING, 2, RING, rows, width), F32),
-        ),
+        out_shape=(jax.ShapeDtypeStruct((rows, width), F32), spread_shape(rows, width)),
         in_specs=[pl.BlockSpec(memory_space=pltpu.VMEM)],
         out_specs=(pl.BlockSpec(memory_space=pltpu.VMEM), pl.BlockSpec(memory_space=pl.ANY)),
         scratch_shapes=reduce_scratch(rows, width)
         + [
+            pltpu.VMEM((rows + CODE_PAD, width), jnp.int16),
             pltpu.SemaphoreType.DMA((copies,)),
             pltpu.SemaphoreType.DMA((copies,)),
             pltpu.SemaphoreType.DMA,
@@ -401,7 +425,217 @@
         compiler_params=pltpu.CompilerParams(collective_id=collective_id, has_side_effects=True),
         name="reduce_and_spread",
     )(part)
-    return share, out.reshape(-1, width)
+
+
+def image_block(tile, codes_ref, out_ref):
+    rows = jnp.concatenate([decode(codes_ref[0, 0, i]) for i in range(RING)], axis=0)
+    part = lax.dot_general(
+        tile, rows, (((0,), (0,)), ((), ())), precision=HIGH, preferred_element_type=F32
+    )
+
+    @pl.when(pl.program_id(0) == 0)
+    def _():
+        out_ref[...] = part
+
+    @pl.when(pl.program_id(0) > 0)
+    def _():
+        out_ref[...] += part
+
+
+def image_kernel(tile_ref, codes_ref, out_ref):
+    image_block(tile_ref[...], codes_ref, out_ref)
+
+
+def update_kernel(scale, tile_ref, codes_ref, kept_rows_ref, kept_cols_ref, new_ref, out_ref):
+    update = lax.dot_general(
+        kept_rows_ref[...], kept_cols_ref[...], (((0,), (0,)), ((), ())), preferred_element_type=F32
+    )
+    tile = tile_ref[...] + update * scale
+    new_ref[...] = tile
+    image_block(tile, codes_ref, out_ref)
+
+
+def image_part(tile, codes, kept=None, scale=None):
+    width = tile.shape[1]
+    height = RING * (codes.shape[3] - CODE_PAD)
+    tile_spec = pl.BlockSpec((height, width), lambda i: (i, 0))
+    code_spec = pl.BlockSpec((1, 1) + codes.shape[2:], lambda i: (i // 2, i % 2, 0, 0, 0))
+    out_spec = pl.BlockSpec((width, codes.shape[4]), lambda i: (0, 0))
+    out_shape = jax.ShapeDtypeStruct((width, codes.shape[4]), F32)
+    if kept is None:
+        return pl.pallas_call(
+            image_kernel,
+            grid=(tile.shape[0] // height,),
+            out_shape=out_shape,
+            in_specs=[tile_spec, code_spec],
+            out_specs=out_spec,
+            name="image",
+        )(tile, codes)
+    kept_rows, kept_cols = kept
+    tokens = kept_rows.shape[0]
+    return pl.pallas_call(
+        functools.partial(update_kernel, scale),
+        grid=(tile.shape[0] // height,),
+        out_shape=(jax.ShapeDtypeStruct(tile.shape, F32), out_shape),
+        in_specs=[
+            tile_spec,
+            code_spec,
+            pl.BlockSpec((tokens, height), lambda i: (0, i)),
+            pl.BlockSpec(kept_cols.shape, lambda i: (0, 0)),
+        ],
+        out_specs=(tile_spec, out_spec),
+        name="update_image",
+    )(tile, codes, kept_rows, kept_cols)
+
+
+def mlp_kernel(
+    hidden_ref, weight_ref, out_ref, hid, weight, part, pair, far1, near1, far2, near2, send, recv, sem
+):
+    place = Place()
+    links = Links(send, recv)
+    load = pltpu.make_async_copy(weight_ref, weight, sem)
+    load.start()
+    meet(plane_neighbours(place) + y_neighbours(place))
+    tokens = hidden_ref.shape[0]
+    width = weight.shape[1]
+    half, piece, tile = width // 2, width // 4, 512
+    up, down = place.ahead("t", 1), place.ahead("t", -1)
+    c = place.c
+    to_up = links.go(hidden_ref, hid.at[place.t], up)
+    to_down = links.go(hidden_ref, hid.at[place.t], down)
+    load.wait()
+
+    def product(group, rows):
+        @pl.loop(0, width // tile)
+        def _(j):
+            cols = pl.ds(pl.multiple_of(j * tile, tile), tile)
+            block = jnp.dot(rows[...], weight[:, cols], preferred_element_type=F32)
+            part[group, :, :, :, cols] = block.reshape(RING, 2, tokens // (2 * RING), tile)
+
+        return links.go(part.at[group, :, 1 - c], pair.at[group], place.other_core())
+
+    pairs = [product(place.t, hidden_ref)]
+    below, above, across = place.along("t", -1), place.along("t", 1), place.along("t", 2)
+    to_up.wait_recv()
+    first = hid.at[below, pl.ds(0, tokens // 2)]
+    on_up = links.go(first, first, up)
+    to_down.wait_recv()
+    second = hid.at[above, pl.ds(tokens // 2, tokens // 2)]
+    on_down = links.go(second, second, down)
+    pairs.append(product(below, hid.at[below]))
+    pairs.append(product(above, hid.at[above]))
+    on_up.wait_recv()
+    on_down.wait_recv()
+    pairs.append(product(across, hid.at[across]))
+    for group, made in zip((place.t, below, above, across), pairs):
+        made.wait_recv()
+
+        @pl.loop(0, RING)
+        def _(i):
+            part[group, i, c] = part[group, i, c] + pair[group, i]
+
+    ways = ((0, "z", "x"), (1, "x", "z"))
+
+    def half_cols(h):
+        return pl.ds(h * half, half)
+
+    def piece_cols(h, d):
+        return pl.ds(h * half + (0 if d > 0 else piece), piece)
+
+    def in_half(d):
+        return pl.ds(0 if d > 0 else piece, piece)
+
+    def line(axis, step, cols, i=slice(None)):
+        if axis == "z":
+            return part.at[place.along("z", step), i, c, :, cols]
+        return part.at[i, place.along("x", step), c, :, cols]
+
+    def block(other, step, cols):
+        if other == "z":
+            return part.at[place.along("z", step), place.x, c, :, cols]
+        return part.at[place.z, place.along("x", step), c, :, cols]
+
+    def add(into, value):
+        into[...] = into[...] + value
+
+    far, early, late = {}, {}, {}
+    for h, axis, _ in ways:
+        for n, d in enumerate((1, -1)):
+            far[h, d] = links.go(line(axis, 2, piece_cols(h, d)), far1.at[h, n], place.ahead(axis, d))
+    for h, axis, _ in ways:
+        for n, d in enumerate((1, -1)):
+            early[h, d] = links.go(
+                line(axis, d, piece_cols(h, -d)), near1.at[h, n, :, :, in_half(-d)], place.ahead(axis, d)
+            )
+    for h, axis, _ in ways:
+        for n, d in enumerate((1, -1)):
+            far[h, d].wait_recv()
+
+            @pl.loop(0, RING)
+            def _(i):
+                add(line(axis, d, piece_cols(h, d), i), far1[h, n, i])
+
+            late[h, d] = links.go(
+                line(axis, d, piece_cols(h, d)), near1.at[h, n, :, :, in_half(d)], place.ahead(axis, d)
+            )
+    for h, axis, other in ways:
+        for d in (1, -1):
+            early[h, d].wait_recv()
+            late[h, d].wait_recv()
+
+        @pl.loop(0, RING)
+        def _(i):
+            add(line(axis, 0, half_cols(h), i), near1[h, 0, i] + near1[h, 1, i])
+
+        for n, d in enumerate((1, -1)):
+            far[h, d] = links.go(block(other, 2, piece_cols(h, d)), far2.at[h, n], place.ahead(other, d))
+        for n, d in enumerate((1, -1)):
+            early[h, d] = links.go(
+                block(other, d, piece_cols(h, -d)), near2.at[h, n, :, in_half(-d)], place.ahead(other, d)
+            )
+    for h, axis, other in ways:
+        for n, d in enumerate((1, -1)):
+            far[h, d].wait_recv()
+            add(block(other, d, piece_cols(h, d)), far2[h, n])
+            late[h, d] = links.go(
+                block(other, d, piece_cols(h, d)), near2.at[h, n, :, in_half(d)], place.ahead(other, d)
+            )
+    for h, axis, other in ways:
+        for d in (1, -1):
+            early[h, d].wait_recv()
+            late[h, d].wait_recv()
+        total = block(other, 0, half_cols(h))[...] + (near2[h, 0] + near2[h, 1])
+        out_ref[:, half_cols(h)] = total.astype(out_ref.dtype)
+    for made in links.started:
+        made.wait_send()
+
+
+def down_projection(hidden, weight, collective_id):
+    tokens, depth = hidden.shape
+    width = weight.shape[1]
+    rows = tokens // (2 * RING)
+    copies = 32
+    return pl.pallas_call(
+        mlp_kernel,
+        out_shape=jax.ShapeDtypeStruct((rows, width), BF16),
+        in_specs=[pl.BlockSpec(memory_space=pltpu.VMEM), pl.BlockSpec(memory_space=pl.ANY)],
+        out_specs=pl.BlockSpec(memory_space=pltpu.VMEM),
+        scratch_shapes=[
+            pltpu.VMEM((RING, tokens, depth), BF16),
+            pltpu.VMEM((depth, width), BF16),
+            pltpu.VMEM((RING, RING, 2, rows, width), F32),
+            pltpu.VMEM((RING, RING, rows, width), F32),
+            pltpu.VMEM((2, 2, RING, rows, width // 4), F32),
+            pltpu.VMEM((2, 2, RING, rows, width // 2), F32),
+            pltpu.VMEM((2, 2, rows, width // 4), F32),
+            pltpu.VMEM((2, 2, rows, width // 2), F32),
+            pltpu.SemaphoreType.DMA((copies,)),
+            pltpu.SemaphoreType.DMA((copies,)),
+            pltpu.SemaphoreType.DMA,
+        ],
+        compiler_params=pltpu.CompilerParams(collective_id=collective_id, has_side_effects=True),
+        name="down_projection",
+    )(hidden, weight)
 
 
 def kept_kernel(kept_ref, rows_ref, cols_ref, send, recv, sem):
@@ -610,35 +844,21 @@
     root = math.sqrt(D)
 
     start_share = lax.dynamic_slice_in_dim(start_basis, t * share_rows, share_rows, 0)
-    start_rows = spread(start_share, 1)
-
-    all_hidden = lax.all_gather(hidden, "tensor", axis=0, tiled=True)
-    mlp_out = lax.psum_scatter(
-        jnp.dot(all_hidden, down_weight, preferred_element_type=F32),
-        "fsdp",
-        scatter_dimension=0,
-        tiled=True,
-    ).astype(BF16)
+    start_codes = spread(start_share, 1)
+
+    mlp_out = down_projection(hidden, down_weight, 0)
     listed = keep_index[0]
     positions = jnp.arange(mlp_out.shape[0], dtype=jnp.int32)
     chosen = (listed[:, None] == positions[None, :]).astype(BF16)
     kept = jnp.dot(chosen, mlp_out, preferred_element_type=F32).astype(BF16)
-    kept_rows, kept_cols = gather_kept(kept, block_width, 2)
-    update = lax.dot_general(
-        kept_rows, kept_cols, (((0,), (0,)), ((), ())), preferred_element_type=F32
-    )
-    new_covariance = covariance + update * (1.0 / total_tokens)
-
-    def image_part(rows):
-        return lax.dot_general(
-            new_covariance, rows, (((0,), (0,)), ((), ())), precision=HIGH, preferred_element_type=F32
-        )
-
-    image_one, image_rows = reduce_and_spread(image_part(start_rows), 3)
+    kept_pair = gather_kept(kept, block_width, 2)
+    new_covariance, part_one = image_part(covariance, start_codes, kept_pair, 1.0 / total_tokens)
+    image_one, codes_one = reduce_and_spread(part_one, 3)
     inverse_one = inverse_factor(total_gram(gram_of(image_one), 4))
-    own_rows = lax.dynamic_slice_in_dim(image_rows, f * share_rows, share_rows, 0)
+    every = codes_one.reshape(fsdp_count, -1, codes_one.shape[-1])
+    own_rows = decode(lax.dynamic_index_in_dim(every, f, 0, keepdims=False))
     first_basis = times_transpose(own_rows, inverse_one, root)
-    image_two = times_transpose(reduce_over_y(image_part(image_rows), 5), inverse_one)
+    image_two = times_transpose(reduce_over_y(image_part(new_covariance, codes_one), 5), inverse_one)
     total_two, whole_two = total_gram(gram_of(image_two), 6, image_two)
     final_basis = times_transpose(whole_two, inverse_factor(total_two), root)
     return (mlp_out, new_covariance, first_basis, final_basis)

time: 551 us -> 478 us (0.87)
  matrix products: 54.3 us -> 13.4 us
  waiting for transfers between devices: 39.8 us -> 0 us
  Pallas kernels: 423 us -> 460 us
  blocking collectives: 14.1 us -> 0 us
  between operations: 14.2 us -> 0.78 us
    pallas_call x1 -> x4, Pallas kernels: 54.8 us -> 124 us  [the longest x1 53 us: down_projection(): pl.pallas_call(mlp_kernel, out_shape=jax.ShapeDtypeStruct((rows, width),...]
    dot_general x4 -> x0, matrix products: 42.1 us -> none  [the longest x2 26.8 us: image_part(): lax.dot_general(new_covariance, rows, (((0,), (0,)), ((), ())), precision...]
    reduce_scatter x1 -> x0, waiting for transfers between devices: 39.8 us -> none  [body(): lax.psum_scatter(jnp.dot(all_hidden, down_weight, preferred_element_type=...]
    pallas_call x1, Pallas kernels: 67.8 us -> 48 us  [reduce_and_spread(): pl.pallas_call(reduce_spread_kernel, out_shape=(jax.ShapeDtypeStruct((row...]
    all_gather x1 -> x0, blocking collectives: 14.1 us -> none  [body(): all_hidden = lax.all_gather(hidden, 'tensor', axis=0, tiled=True)]
    pallas_call x2, Pallas kernels: 197 us -> 187 us  [inverse_factor(): pl.pallas_call(inverse_factor_kernel, out_shape=jax.ShapeDtypeStruct((n,...]
  transfers between devices with their start and end apart: 1 -> 0, of which waited for: 1 -> 0; matrix products, arithmetic and copies ran while one was open for 0% -> 0% of each run, Pallas kernels for 10% -> 0%
where the time goes in v3:
time: 478 us; the launch traced here: 477 us
  Pallas kernels  460 us (96%)
  matrix products  13.4 us (3%)
    pallas_call x2, Pallas kernels, inverse_factor(): pl.pallas_call(inverse_factor_kernel, out_shape=jax.ShapeDtypeStruct((n,...  187 us
    pallas_call x2, Pallas kernels, total_gram(): pl.pallas_call(functools.partial(total_kernel, rows is not None), out_sha...  60 us
    pallas_call x1, Pallas kernels, down_projection(): pl.pallas_call(mlp_kernel, out_shape=jax.ShapeDtypeStruct((rows, width),...  53 us
    pallas_call x1, Pallas kernels, reduce_and_spread(): pl.pallas_call(reduce_spread_kernel, out_shape=(jax.ShapeDtypeStruct((row...  48 us
    pallas_call x1, Pallas kernels, spread(): pl.pallas_call(spread_kernel, out_shape=spread_shape(rows, width), in_spe...  43 us
    pallas_call x1, Pallas kernels, gather_kept(): pl.pallas_call(kept_kernel, out_shape=(jax.ShapeDtypeStruct(lead + (width...  27.6 us
    pallas_call x1, Pallas kernels, image_part(): pl.pallas_call(functools.partial(update_kernel, scale), grid=(tile.shape[...  15.6 us
    pallas_call x1, Pallas kernels, reduce_over_y(): pl.pallas_call(reduce_kernel, out_shape=jax.ShapeDtypeStruct((rows, width...  13.9 us

profile of v3, /device:TPU:1, one launch (start us, length us, event | category | flops | bytes accessed | tf_op | source)
XLA Modules:
  0.0 477.0 jit_solution(1140932192840735067)
XLA Ops:
  0.6 0.0 copy-start
  0.6 0.0 copy-start.5
  0.7 53.0 %down_projection.1 = bf16[16,4096]{1,0:T(8,128)(2,1)} custom-call(bf16[128,896]{1,0:T(8,128)(2,1)} %hidden_ref.1, bf16[896,4096]{1,0:T(8,128)(2,1)} %weight_ref.1), custom_call_target="tpu_custom_call" | custom-call | tf_op jit(solution)/shard_map/down_projection/pallas_call | solution.py:618
  53.7 0.0 copy-done.5
  53.7 1.7 convolution_convert_fusion.kept_ref
  55.5 0.0 copy-done
  55.5 0.7 constant_dynamic-slice_fusion.share_ref
  56.2 27.6 %gather_kept.1 = (bf16[4,4,2,8,4096]{4,3,2,1,0:T(8,128)(2,1)}, bf16[4,4,2,8,512]{4,3,2,1,0:T(8,128)(2,1)}) custom-call(bf16[8,4096]{1,0:T(8,128)(2,1)} %convolution_convert_fusion.kept_ref), custom_call_target="tpu_custom_call" | custom-call | tf_op jit(solution)/shard_map/gather_kept/pallas_call | solution.py:696
  83.8 43.0 %spread.1.codes_ref = s16[4,2,4,144,512]{4,3,2,1,0:T(8,128)(2,1)} custom-call(f32[128,512]{1,0:T(8,128)} %constant_dynamic-slice_fusion.share_ref), custom_call_target="tpu_custom_call" | custom-call | tf_op jit(solution)/shard_map/spread/pallas_call | solution.py:322
  126.8 15.6 %update_image.1 = (f32[4096,512]{1,0:T(8,128)}, f32[512,512]{1,0:T(8,128)}) custom-call(f32[4096,512]{1,0:T(8,128)} %tile_ref.1, s16[4,2,4,144,512]{4,3,2,1,0:T(8,128)(2,1)} %spread.1.codes_ref, bf16[256,4096]{1,0:T(8,128)(2,1)} %bitcast.22, bf16[256,512]{1,0:T(8,128)(2,1)} %bitcast.24), custom_call_target="tpu_custom_call" | custom-call | tf_op jit(solution)/shard_map/update_image/pallas_call | solution.py:476
  142.4 48.0 %reduce_and_spread.1 = (f32[128,512]{1,0:T(8,128)}, s16[4,2,4,144,512]{4,3,2,1,0:T(8,128)(2,1)}) custom-call(f32[512,512]{1,0:T(8,128)} %get-tuple-element.15.part_ref), custom_call_target="tpu_custom_call" | custom-call | tf_op jit(solution)/shard_map/reduce_and_spread/pallas_call | solution.py:413
  190.4 1.0 convert_convert_fusion
  191.4 2.6 fusion.5.refs_0_
  194.0 29.8 %total_gram.2.gram_ref = f32[512,512]{1,0:T(8,128)} custom-call(f32[512,512]{1,0:T(8,128)} %fusion.5.refs_0_), custom_call_target="tpu_custom_call" | custom-call | tf_op jit(solution)/shard_map/total_gram/pallas_call | solution.py:813
  223.8 178.0 %inverse_factor.2 = f32[512,512]{1,0:T(8,128)} custom-call(f32[512,512]{1,0:T(8,128)} %total_gram.2.gram_ref), custom_call_target="tpu_custom_call" | custom-call | flops 8000000000 | bytes 2097152 | tf_op jit(solution)/shard_map/inverse_factor/pallas_call | solution.py:83
  401.9 2.6 convolution_multiply_fusion.1
  404.4 12.5 %image.1.part_ref = f32[512,512]{1,0:T(8,128)} custom-call(f32[4096,512]{1,0:T(8,128)} %get-tuple-element.25.tile_ref, s16[4,2,4,144,512]{4,3,2,1,0:T(8,128)(2,1)} %get-tuple-element.16.codes_ref), custom_call_target="tpu_custom_call" | custom-call | tf_op jit(solution)/shard_map/image/pallas_call | solution.py:466
  416.9 13.9 %reduce_over_y.1 = f32[128,512]{1,0:T(8,128)} custom-call(f32[512,512]{1,0:T(8,128)} %image.1.part_ref), custom_call_target="tpu_custom_call" | custom-call | tf_op jit(solution)/shard_map/reduce_over_y/pallas_call | solution.py:389
  430.8 1.6 fusion.6.refs_1_
  432.5 1.6 fusion.7.refs_0_
  434.0 30.2 %total_gram.3 = (f32[512,512]{1,0:T(8,128)}, f32[4,128,512]{2,1,0:T(8,128)}) custom-call(f32[512,512]{1,0:T(8,128)} %fusion.7.refs_0_, f32[128,512]{1,0:T(8,128)} %copy-done.1), custom_call_target="tpu_custom_call" | custom-call | tf_op jit(solution)/shard_map/total_gram/pallas_call | solution.py:813
  464.3 8.8 %inverse_factor.3 = f32[512,512]{1,0:T(8,128)} custom-call(f32[512,512]{1,0:T(8,128)} %get-tuple-element.19.gram_ref), custom_call_target="tpu_custom_call" | custom-call | flops 8000000000 | bytes 2097152 | tf_op jit(solution)/shard_map/inverse_factor/pallas_call | solution.py:83
  473.1 3.2 convolution_multiply_fusion
  476.3 0.7 copy.10
  (9 shorter events, 0.0 us)
Async XLA Ops:
  0.6 54.8 %copy-start = (f32[512,512]{1,0:T(8,128)S(1)}, f32[512,512]{1,0:T(8,128)}, u32[]{:S(2)}) copy-start(f32[512,512]{1,0:T(8,128)} %param.9) | copy-start | bytes 3145732
  0.6 53.1 %copy-start.5 = (s32[1,8]{1,0:T(1,128)S(1)}, s32[1,8]{1,0:T(1,128)}, u32[]{:S(2)}) copy-start(s32[1,8]{1,0:T(1,128)} %param.8) | copy-start | bytes 100
  404.4 26.4 %copy-start.2 = (f32[512,512]{1,0:T(8,128)S(1)}, f32[512,512]{1,0:T(8,128)}, u32[]{:S(2)}) copy-start(f32[512,512]{1,0:T(8,128)} %inverse_factor.2) | copy-start | bytes 3145732
  432.4 1.6 copy-start.1
  464.3 8.8 %copy-start.4 = (f32[4,128,512]{2,1,0:T(8,128)S(1)}, f32[4,128,512]{2,1,0:T(8,128)}, u32[]{:S(2)}) copy-start(f32[4,128,512]{2,1,0:T(8,128)} %get-tuple-element.18) | copy-start | bytes 3145732
  464.3 12.0 %copy-start.3 = (bf16[16,4096]{1,0:T(8,128)(2,1)S(1)}, bf16[16,4096]{1,0:T(8,128)(2,1)}, u32[]{:S(2)}) copy-start(bf16[16,4096]{1,0:T(8,128)(2,1)} %down_projection.1) | copy-start | bytes 393220

commit v4 on v3

--- a/solution.py
+++ b/solution.py
@@ -96,12 +96,6 @@
         rows, factor, (((1,), (1,)), ((), ())), precision=HIGH, preferred_element_type=F32
     )
     return out * scale if scale != 1.0 else out
-
-
-def gram_of(rows):
-    return lax.dot_general(
-        rows, rows, (((0,), (0,)), ((), ())), precision=HIGH, preferred_element_type=F32
-    )
 
 
 MESH = pl.DeviceIdType.MESH
@@ -170,7 +164,7 @@
         return made
 
 
-def gather_plane(own, out, slot, width, links, place):
+def gather_steps(own, out, slot, width, links, place):
     half, piece = width // 2, width // 4
     ways = ((0, "x", "z"), (1, "z", "x"))
 
@@ -193,43 +187,48 @@
     def piece_cols(h, d):
         return pl.ds(h * half + (0 if d > 0 else piece), piece)
 
-    first, second, third, fourth, rest = {}, {}, {}, {}, []
+    made, rest = {}, []
     for h, axis, _ in ways:
         for d in (1, -1):
             cols = half_cols(h)
-            first[h, d] = links.go(own.at[:, cols], spot(axis, 0, cols), place.ahead(axis, d))
+            made[h, d] = links.go(own.at[:, cols], spot(axis, 0, cols), place.ahead(axis, d))
+    yield
+    onward = {}
     for h, axis, _ in ways:
         for d in (1, -1):
-            first[h, d].wait_recv()
-            cols = piece_cols(h, d)
-            chunk = spot(axis, -d, cols)
-            second[h, d] = links.go(chunk, chunk, place.ahead(axis, d))
-    return ways, line, half_cols, piece_cols, second, third, fourth, rest
-
-
-def finish_plane(parts, links, place):
-    ways, line, half_cols, piece_cols, second, third, fourth, rest = parts
+            made[h, d].wait_recv()
+            chunk = spot(axis, -d, piece_cols(h, d))
+            onward[h, d] = links.go(chunk, chunk, place.ahead(axis, d))
+    yield
     for h, axis, other in ways:
         for d in (1, -1):
-            second[h, d].wait_recv()
+            onward[h, d].wait_recv()
         whole = line(axis, other, 0, half_cols(h))
         for d in (1, -1):
-            third[h, d] = links.go(whole, whole, place.ahead(other, d))
+            made[h, d] = links.go(whole, whole, place.ahead(other, d))
         rest.append(links.go(whole, whole, place.other_core()))
+    yield
     for h, axis, other in ways:
         for d in (1, -1):
-            third[h, d].wait_recv()
+            made[h, d].wait_recv()
             part = line(axis, other, -d, piece_cols(h, d))
-            fourth[h, d] = links.go(part, part, place.ahead(other, d))
+            onward[h, d] = links.go(part, part, place.ahead(other, d))
             whole = line(axis, other, -d, half_cols(h))
             rest.append(links.go(whole, whole, place.other_core()))
+    yield
     for h, axis, other in ways:
         for d in (1, -1):
-            fourth[h, d].wait_recv()
+            onward[h, d].wait_recv()
             part = line(axis, other, -2 * d, piece_cols(h, d))
             rest.append(links.go(part, part, place.other_core()))
-    for made in rest:
-        made.wait_recv()
+    yield
+    for made_last in rest:
+        made_last.wait_recv()
+
+
+def run(steps):
+    for _ in steps:
+        pass
 
 
 GATHER_COPIES = 26
@@ -247,28 +246,38 @@
     return (z, x, c)
 
 
-def swap_in(share, out, links, place, sem):
+def swap_start(share, out, links, place, sem):
     sent = links.copy(
         share, out.at[by_column(place.t, place.x, place.c)], place.device(z=place.t, t=place.z)
     )
+    kept = pltpu.make_async_copy(share, out.at[by_column(place.z, place.x, place.c)], sem)
 
     @pl.when(place.t != place.z)
     def _():
         sent.start()
+
+    @pl.when(place.t == place.z)
+    def _():
+        kept.start()
+
+    return sent, kept
+
+
+def swap_end(swap, place):
+    sent, kept = swap
+
+    @pl.when(place.t != place.z)
+    def _():
         sent.wait_recv()
 
     @pl.when(place.t == place.z)
     def _():
-        kept = pltpu.make_async_copy(share, out.at[by_column(place.z, place.x, place.c)], sem)
-        kept.start()
         kept.wait()
 
-    return sent
-
-
-def settle(links, place, swapped):
+
+def settle(links, place, swap=None):
     for made in links.started:
-        if made is swapped:
+        if swap is not None and made is swap[0]:
 
             @pl.when(place.t != place.z)
             def _():
@@ -297,42 +306,13 @@
     return wide[:rows] * jnp.exp2(wide[rows : rows + 1])
 
 
-def spread_codes(codes, out_ref, links, place, sem):
-    swapped = swap_in(codes, out_ref, links, place, sem)
-    own = out_ref.at[by_column(place.z, place.x, place.c)]
-    parts = gather_plane(own, out_ref, by_column, codes.shape[1], links, place)
-    finish_plane(parts, links, place)
-    settle(links, place, swapped)
-
-
-def spread_kernel(share_ref, out_ref, codes, send, recv, sem):
-    place = Place()
-    links = Links(send, recv)
-    meet(plane_neighbours(place), place)
-    encode(share_ref[...], codes)
-    spread_codes(codes, out_ref, links, place, sem)
-
-
 def spread_shape(rows, width):
     return jax.ShapeDtypeStruct((RING, 2, RING, rows + CODE_PAD, width), jnp.int16)
 
 
-def spread(share, collective_id):
-    rows, width = share.shape
-    return pl.pallas_call(
-        spread_kernel,
-        out_shape=spread_shape(rows, width),
-        in_specs=[pl.BlockSpec(memory_space=pltpu.VMEM)],
-        out_specs=pl.BlockSpec(memory_space=pl.ANY),
-        scratch_shapes=[
-            pltpu.VMEM((rows + CODE_PAD, width), jnp.int16),
-            pltpu.SemaphoreType.DMA((GATHER_COPIES + 1,)),
-            pltpu.SemaphoreType.DMA((GATHER_COPIES + 1,)),
-            pltpu.SemaphoreType.DMA,
-        ],
-        compiler_params=pltpu.CompilerParams(collective_id=collective_id, has_side_effects=True),
-        name="spread",
-    )(share)
+def spread_steps(codes, out_ref, links, place):
+    own = out_ref.at[by_column(place.z, place.x, place.c)]
+    return gather_steps(own, out_ref, by_column, codes.shape[1], links, place)
 
 
 def reduce_y(part_ref, share_ref, relay, build, arrive, links, place):
@@ -373,58 +353,6 @@
 
 def y_neighbours(place):
     return [place.ahead("t", 1), place.ahead("t", -1)]
-
-
-def reduce_kernel(part_ref, share_ref, relay, build, arrive, send, recv):
-    place = Place()
-    links = Links(send, recv)
-    meet(y_neighbours(place))
-    reduce_y(part_ref, share_ref, relay, build, arrive, links, place)
-    for made in links.started:
-        made.wait_send()
-
-
-def reduce_over_y(part, collective_id):
-    rows, width = part.shape[0] // RING, part.shape[1]
-    return pl.pallas_call(
-        reduce_kernel,
-        out_shape=jax.ShapeDtypeStruct((rows, width), F32),
-        in_specs=[pl.BlockSpec(memory_space=pltpu.VMEM)],
-        out_specs=pl.BlockSpec(memory_space=pltpu.VMEM),
-        scratch_shapes=reduce_scratch(rows, width)
-        + [pltpu.SemaphoreType.DMA((REDUCE_COPIES,)), pltpu.SemaphoreType.DMA((REDUCE_COPIES,))],
-        compiler_params=pltpu.CompilerParams(collective_id=collective_id, has_side_effects=True),
-        name="reduce_over_y",
-    )(part)
-
-
-def reduce_spread_kernel(part_ref, share_ref, out_ref, relay, build, arrive, codes, send, recv, sem):
-    place = Place()
-    links = Links(send, recv)
-    meet(plane_neighbours(place) + y_neighbours(place), place)
-    reduce_y(part_ref, share_ref, relay, build, arrive, links, place)
-    share_ref[...] = encode(share_ref[...], codes)
-    spread_codes(codes, out_ref, links, place, sem)
-
-
-def reduce_and_spread(part, collective_id):
-    rows, width = part.shape[0] // RING, part.shape[1]
-    copies = REDUCE_COPIES + 1 + GATHER_COPIES
-    return pl.pallas_call(
-        reduce_spread_kernel,
-        out_shape=(jax.ShapeDtypeStruct((rows, width), F32), spread_shape(rows, width)),
-        in_specs=[pl.BlockSpec(memory_space=pltpu.VMEM)],
-        out_specs=(pl.BlockSpec(memory_space=pltpu.VMEM), pl.BlockSpec(memory_space=pl.ANY)),
-        scratch_shapes=reduce_scratch(rows, width)
-        + [
-            pltpu.VMEM((rows + CODE_PAD, width), jnp.int16),
-            pltpu.SemaphoreType.DMA((copies,)),
-            pltpu.SemaphoreType.DMA((copies,)),
-            pltpu.SemaphoreType.DMA,
-        ],
-        compiler_params=pltpu.CompilerParams(collective_id=collective_id, has_side_effects=True),
-        name="reduce_and_spread",
-    )(part)
 
 
 def image_block(tile, codes_ref, out_ref):
@@ -489,13 +417,33 @@
 
 
 def mlp_kernel(
-    hidden_ref, weight_ref, out_ref, hid, weight, part, pair, far1, near1, far2, near2, send, recv, sem
+    hidden_ref,
+    weight_ref,
+    start_ref,
+    out_ref,
+    spread_ref,
+    hid,
+    weight,
+    part,
+    pair,
+    far1,
+    near1,
+    far2,
+    near2,
+    codes,
+    send,
+    recv,
+    sem,
+    swap_sem,
 ):
     place = Place()
     links = Links(send, recv)
     load = pltpu.make_async_copy(weight_ref, weight, sem)
     load.start()
-    meet(plane_neighbours(place) + y_neighbours(place))
+    share_rows = codes.shape[0] - CODE_PAD
+    share_start = pl.multiple_of(place.t * share_rows, share_rows)
+    encode(start_ref[pl.ds(share_start, share_rows), :], codes)
+    meet(plane_neighbours(place) + y_neighbours(place), place)
     tokens = hidden_ref.shape[0]
     width = weight.shape[1]
     half, piece, tile = width // 2, width // 4, 512
@@ -503,6 +451,7 @@
     c = place.c
     to_up = links.go(hidden_ref, hid.at[place.t], up)
     to_down = links.go(hidden_ref, hid.at[place.t], down)
+    swap = swap_start(codes, spread_ref, links, place, swap_sem)
     load.wait()
 
     def product(group, rows):
@@ -515,6 +464,9 @@
         return links.go(part.at[group, :, 1 - c], pair.at[group], place.other_core())
 
     pairs = [product(place.t, hidden_ref)]
+    swap_end(swap, place)
+    spread = spread_steps(codes, spread_ref, links, place)
+    next(spread)
     below, above, across = place.along("t", -1), place.along("t", 1), place.along("t", 2)
     to_up.wait_recv()
     first = hid.at[below, pl.ds(0, tokens // 2)]
@@ -522,11 +474,14 @@
     to_down.wait_recv()
     second = hid.at[above, pl.ds(tokens // 2, tokens // 2)]
     on_down = links.go(second, second, down)
+    next(spread)
     pairs.append(product(below, hid.at[below]))
+    next(spread)
     pairs.append(product(above, hid.at[above]))
     on_up.wait_recv()
     on_down.wait_recv()
     pairs.append(product(across, hid.at[across]))
+    next(spread)
     for group, made in zip((place.t, below, above, across), pairs):
         made.wait_recv()
 
@@ -534,6 +489,7 @@
         def _(i):
             part[group, i, c] = part[group, i, c] + pair[group, i]
 
+    next(spread)
     ways = ((0, "z", "x"), (1, "x", "z"))
 
     def half_cols(h):
@@ -606,20 +562,22 @@
             late[h, d].wait_recv()
         total = block(other, 0, half_cols(h))[...] + (near2[h, 0] + near2[h, 1])
         out_ref[:, half_cols(h)] = total.astype(out_ref.dtype)
-    for made in links.started:
-        made.wait_send()
-
-
-def down_projection(hidden, weight, collective_id):
+    run(spread)
+    settle(links, place, swap)
+
+
+def down_projection(hidden, weight, start, collective_id):
     tokens, depth = hidden.shape
     width = weight.shape[1]
     rows = tokens // (2 * RING)
-    copies = 32
+    share_rows, rank = start.shape[0] // RING, start.shape[1]
+    copies = 32 + 1 + GATHER_COPIES
+    vmem, anywhere = pl.BlockSpec(memory_space=pltpu.VMEM), pl.BlockSpec(memory_space=pl.ANY)
     return pl.pallas_call(
         mlp_kernel,
-        out_shape=jax.ShapeDtypeStruct((rows, width), BF16),
-        in_specs=[pl.BlockSpec(memory_space=pltpu.VMEM), pl.BlockSpec(memory_space=pl.ANY)],
-        out_specs=pl.BlockSpec(memory_space=pltpu.VMEM),
+        out_shape=(jax.ShapeDtypeStruct((rows, width), BF16), spread_shape(share_rows, rank)),
+        in_specs=[vmem, anywhere, vmem],
+        out_specs=(vmem, anywhere),
         scratch_shapes=[
             pltpu.VMEM((RING, tokens, depth), BF16),
             pltpu.VMEM((depth, width), BF16),
@@ -629,13 +587,15 @@
             pltpu.VMEM((2, 2, RING, rows, width // 2), F32),
             pltpu.VMEM((2, 2, rows, width // 4), F32),
             pltpu.VMEM((2, 2, rows, width // 2), F32),
+            pltpu.VMEM((share_rows + CODE_PAD, rank), jnp.int16),
             pltpu.SemaphoreType.DMA((copies,)),
             pltpu.SemaphoreType.DMA((copies,)),
+            pltpu.SemaphoreType.DMA,
             pltpu.SemaphoreType.DMA,
         ],
         compiler_params=pltpu.CompilerParams(collective_id=collective_id, has_side_effects=True),
         name="down_projection",
-    )(hidden, weight)
+    )(hidden, weight, start)
 
 
 def kept_kernel(kept_ref, rows_ref, cols_ref, send, recv, sem):
@@ -644,9 +604,11 @@
     meet(plane_neighbours(place) + y_neighbours(place))
     local = pltpu.make_async_copy(kept_ref, rows_ref.at[by_token(place.z, place.x, place.c)], sem)
     local.start()
-    parts = gather_plane(kept_ref, rows_ref, by_token, kept_ref.shape[1], links, place)
+    steps = gather_steps(kept_ref, rows_ref, by_token, kept_ref.shape[1], links, place)
+    next(steps)
+    next(steps)
     local.wait()
-    finish_plane(parts, links, place)
+    run(steps)
     for made in links.started:
         made.wait_send()
     width = cols_ref.shape[-1]
@@ -712,32 +674,16 @@
     return kept_rows.reshape(-1, width), kept_cols.reshape(-1, tile_width)
 
 
-def total_kernel(with_rows, *refs):
-    if with_rows:
-        gram_ref, rows_ref, out_ref, all_ref = refs[:4]
-        refs = refs[4:]
-    else:
-        gram_ref, out_ref = refs[:2]
-        refs = refs[2:]
-    pair, mine, first, second, last, sum_one, sum_two, send, recv = refs
-    place = Place()
-    links = Links(send, recv)
+def total_steps(gram_ref, out_ref, scratch, links, place):
+    pair, mine, first, second, last, sum_one, sum_two = scratch
     n = gram_ref.shape[0]
     half, width = n // 2, n // 2
     block, piece = half // RING, half // RING // RING
     ways = (("x", "z", pl.ds(0, width)), ("z", "x", pl.ds(width, width)))
-    meet(
-        [place.other_core()]
-        + [place.ahead(axis, k) for axis in ("x", "z", "t") for k in (1, 2, 3)]
-    )
     kept_base = pl.multiple_of(place.c * half, half)
     gone_base = pl.multiple_of((1 - place.c) * half, half)
     swapped = links.go(gram_ref.at[pl.ds(gone_base, half)], pair, place.other_core())
-    relayed = []
-    if with_rows:
-        around = all_ref.at[place.t]
-        relayed = [links.go(rows_ref, around, place.ahead("t", d)) for d in (1, -1)]
-        all_ref[pl.ds(place.t, 1)] = rows_ref[...][None]
+    yield
     swapped.wait_recv()
     mine[...] = gram_ref[pl.ds(kept_base, half), :] + pair[...]
     sent = {}
@@ -747,6 +693,7 @@
             sent[p, k] = links.go(
                 mine.at[pl.ds(start, block), cols], first.at[p, k - 1], place.ahead(axis, k)
             )
+    yield
     for p, (axis, other, cols) in enumerate(ways):
         for k in (1, 2, 3):
             sent[p, k].wait_recv()
@@ -757,6 +704,7 @@
             sent[p, k] = links.go(
                 sum_one.at[p, pl.ds(start, piece)], second.at[p, k - 1], place.ahead(other, k)
             )
+    yield
     for p, (axis, other, cols) in enumerate(ways):
         for k in (1, 2, 3):
             sent[p, k].wait_recv()
@@ -765,6 +713,7 @@
         for k in (1, 2, 3):
             sent[p, k] = links.go(sum_two.at[p], last.at[p, place.t], place.ahead("t", k))
         last[p, pl.ds(place.t, 1)] = sum_two[p][None]
+    yield
     for p, (axis, other, cols) in enumerate(ways):
         for k in (1, 2, 3):
             sent[p, k].wait_recv()
@@ -774,13 +723,7 @@
         final[...] = (last[p, 0] + last[p, 1]) + (last[p, 2] + last[p, 3])
         for k in (1, 2, 3):
             sent[p, k] = links.go(final, final, place.ahead(other, k))
-    if with_rows:
-        part = rows_ref.shape[0] // 2
-        onward = []
-        for d, made in zip((1, -1), relayed):
-            made.wait_recv()
-            held = all_ref.at[place.along("t", -d), pl.ds(0 if d > 0 else part, part)]
-            onward.append(links.go(held, held, place.ahead("t", d)))
+    yield
     for p, (axis, other, cols) in enumerate(ways):
         for k in (1, 2, 3):
             sent[p, k].wait_recv()
@@ -788,78 +731,173 @@
         whole = out_ref.at[pl.ds(start, block), cols]
         for k in (1, 2, 3):
             sent[p, k] = links.go(whole, whole, place.ahead(axis, k))
+    yield
     for p in range(2):
         for k in (1, 2, 3):
             sent[p, k].wait_recv()
     side = out_ref.at[pl.ds(kept_base, half)]
-    links.go(side, side, place.other_core()).wait_recv()
-    if with_rows:
-        for made in onward:
-            made.wait_recv()
-    for made in links.started:
-        made.wait_send()
-
-
-def total_gram(gram, collective_id, rows=None):
-    n = gram.shape[0]
+    across = links.go(side, side, place.other_core())
+    yield
+    across.wait_recv()
+
+
+TOTAL_COPIES = 32
+
+
+def total_scratch(n):
     block, piece = n // 2 // RING, n // 2 // RING // RING
-    copies = 2 + 30 + (4 if rows is not None else 0)
-    shapes = [jax.ShapeDtypeStruct((n, n), F32)]
-    operands = [gram]
-    if rows is not None:
-        shapes.append(jax.ShapeDtypeStruct((RING,) + rows.shape, F32))
-        operands.append(rows)
+    return [
+        pltpu.VMEM((n // 2, n), F32),
+        pltpu.VMEM((n // 2, n), F32),
+        pltpu.VMEM((2, 3, block, n // 2), F32),
+        pltpu.VMEM((2, 3, piece, n // 2), F32),
+        pltpu.VMEM((2, RING, piece, n // 2), F32),
+        pltpu.VMEM((2, block, n // 2), F32),
+        pltpu.VMEM((2, piece, n // 2), F32),
+    ]
+
+
+def everyone(place):
+    return [place.other_core()] + [
+        place.ahead(axis, k) for axis in ("x", "z", "t") for k in (1, 2, 3)
+    ]
+
+
+def gram_of(rows):
+    return lax.dot_general(
+        rows, rows, (((0,), (0,)), ((), ())), precision=HIGH, preferred_element_type=F32
+    )
+
+
+def first_image_kernel(part_ref, out_ref, total_ref, share, gram, codes, *refs):
+    relay, build, arrive = refs[:3]
+    scratch = refs[3:10]
+    send, recv, sem = refs[10:]
+    place = Place()
+    links = Links(send, recv)
+    meet(everyone(place), place)
+    reduce_y(part_ref, share, relay, build, arrive, links, place)
+    known = encode(share[...], codes)
+    swap = swap_start(codes, out_ref, links, place, sem)
+    gram[...] = gram_of(known)
+    total = total_steps(gram, total_ref, scratch, links, place)
+    next(total)
+    swap_end(swap, place)
+    spread = spread_steps(codes, out_ref, links, place)
+    next(spread)
+    next(total)
+    next(spread)
+    next(total)
+    next(spread)
+    next(total)
+    next(total)
+    next(spread)
+    next(total)
+    next(spread)
+    run(total)
+    run(spread)
+    settle(links, place, swap)
+
+
+def first_image(part, collective_id):
+    rows, width = part.shape[0] // RING, part.shape[1]
+    copies = REDUCE_COPIES + 1 + GATHER_COPIES + TOTAL_COPIES
     vmem = pl.BlockSpec(memory_space=pltpu.VMEM)
-    out = pl.pallas_call(
-        functools.partial(total_kernel, rows is not None),
-        out_shape=tuple(shapes),
-        in_specs=[vmem] * len(operands),
-        out_specs=tuple([vmem] * len(shapes)),
+    return pl.pallas_call(
+        first_image_kernel,
+        out_shape=(spread_shape(rows, width), jax.ShapeDtypeStruct((width, width), F32)),
+        in_specs=[vmem],
+        out_specs=(pl.BlockSpec(memory_space=pl.ANY), vmem),
         scratch_shapes=[
-            pltpu.VMEM((n // 2, n), F32),
-            pltpu.VMEM((n // 2, n), F32),
-            pltpu.VMEM((2, 3, block, n // 2), F32),
-            pltpu.VMEM((2, 3, piece, n // 2), F32),
-            pltpu.VMEM((2, RING, piece, n // 2), F32),
-            pltpu.VMEM((2, block, n // 2), F32),
-            pltpu.VMEM((2, piece, n // 2), F32),
+            pltpu.VMEM((rows, width), F32),
+            pltpu.VMEM((width, width), F32),
+            pltpu.VMEM((rows + CODE_PAD, width), jnp.int16),
+        ]
+        + reduce_scratch(rows, width)
+        + total_scratch(width)
+        + [
             pltpu.SemaphoreType.DMA((copies,)),
             pltpu.SemaphoreType.DMA((copies,)),
+            pltpu.SemaphoreType.DMA,
         ],
         compiler_params=pltpu.CompilerParams(collective_id=collective_id, has_side_effects=True),
-        name="total_gram",
-    )(*operands)
-    if rows is None:
-        return out[0]
-    return out[0], out[1].reshape(-1, rows.shape[1])
+        name="first_image",
+    )(part)
+
+
+def second_image_kernel(part_ref, inverse_ref, rows_ref, total_ref, share, gram, *refs):
+    relay, build, arrive = refs[:3]
+    scratch = refs[3:10]
+    send, recv = refs[10:]
+    place = Place()
+    links = Links(send, recv)
+    meet(everyone(place))
+    reduce_y(part_ref, share, relay, build, arrive, links, place)
+    image = times_transpose(share[...], inverse_ref[...])
+    rows_ref[pl.ds(place.t, 1)] = image[None]
+    gram[...] = gram_of(image)
+    total = total_steps(gram, total_ref, scratch, links, place)
+    next(total)
+    next(total)
+    own = rows_ref.at[place.t]
+    around = [links.go(own, own, place.ahead("t", d)) for d in (1, -1)]
+    next(total)
+    next(total)
+    next(total)
+    half = image.shape[0] // 2
+    onward = []
+    for d, made in zip((1, -1), around):
+        made.wait_recv()
+        held = rows_ref.at[place.along("t", -d), pl.ds(0 if d > 0 else half, half)]
+        onward.append(links.go(held, held, place.ahead("t", d)))
+    run(total)
+    for made in onward:
+        made.wait_recv()
+    settle(links, place)
+
+
+def second_image(part, inverse, collective_id):
+    rows, width = part.shape[0] // RING, part.shape[1]
+    copies = REDUCE_COPIES + TOTAL_COPIES + 4
+    vmem = pl.BlockSpec(memory_space=pltpu.VMEM)
+    out, total = pl.pallas_call(
+        second_image_kernel,
+        out_shape=(
+            jax.ShapeDtypeStruct((RING, rows, width), F32),
+            jax.ShapeDtypeStruct((width, width), F32),
+        ),
+        in_specs=[vmem, vmem],
+        out_specs=(vmem, vmem),
+        scratch_shapes=[pltpu.VMEM((rows, width), F32), pltpu.VMEM((width, width), F32)]
+        + reduce_scratch(rows, width)
+        + total_scratch(width)
+        + [pltpu.SemaphoreType.DMA((copies,)), pltpu.SemaphoreType.DMA((copies,))],
+        compiler_params=pltpu.CompilerParams(collective_id=collective_id, has_side_effects=True),
+        name="second_image",
+    )(part, inverse)
+    return out.reshape(-1, width), total
 
 
 def body(hidden, down_weight, covariance, keep_index, start_basis):
     fsdp_count = lax.axis_size("fsdp")
     total_tokens = TOK_DEV * fsdp_count
-    quarter, block_width = covariance.shape
-    share_rows = quarter // fsdp_count
+    block_width = covariance.shape[1]
     f = lax.axis_index("fsdp")
-    t = lax.axis_index("tensor")
     root = math.sqrt(D)
 
-    start_share = lax.dynamic_slice_in_dim(start_basis, t * share_rows, share_rows, 0)
-    start_codes = spread(start_share, 1)
-
-    mlp_out = down_projection(hidden, down_weight, 0)
+    mlp_out, start_codes = down_projection(hidden, down_weight, start_basis, 0)
     listed = keep_index[0]
     positions = jnp.arange(mlp_out.shape[0], dtype=jnp.int32)
     chosen = (listed[:, None] == positions[None, :]).astype(BF16)
     kept = jnp.dot(chosen, mlp_out, preferred_element_type=F32).astype(BF16)
     kept_pair = gather_kept(kept, block_width, 2)
     new_covariance, part_one = image_part(covariance, start_codes, kept_pair, 1.0 / total_tokens)
-    image_one, codes_one = reduce_and_spread(part_one, 3)
-    inverse_one = inverse_factor(total_gram(gram_of(image_one), 4))
+    codes_one, total_one = first_image(part_one, 1)
+    inverse_one = inverse_factor(total_one)
     every = codes_one.reshape(fsdp_count, -1, codes_one.shape[-1])
     own_rows = decode(lax.dynamic_index_in_dim(every, f, 0, keepdims=False))
     first_basis = times_transpose(own_rows, inverse_one, root)
-    image_two = times_transpose(reduce_over_y(image_part(new_covariance, codes_one), 5), inverse_one)
-    total_two, whole_two = total_gram(gram_of(image_two), 6, image_two)
+    whole_two, total_two = second_image(image_part(new_covariance, codes_one), inverse_one, 3)
     final_basis = times_transpose(whole_two, inverse_factor(total_two), root)
     return (mlp_out, new_covariance, first_basis, final_basis)
 

time: 478 us -> 426 us (0.89)
  Pallas kernels: 460 us -> 415 us
  matrix products: 13.4 us -> 7.55 us
    pallas_call x6 -> x3, Pallas kernels: 218 us -> 166 us  [the longest x1 65.2 us: down_projection(): pl.pallas_call(mlp_kernel, out_shape=(jax.ShapeDtypeStruct((rows, width),...]
    pallas_call x1, Pallas kernels: 27.6 us -> 34.7 us  [gather_kept(): pl.pallas_call(kept_kernel, out_shape=(jax.ShapeDtypeStruct(lead + (width...]
where the time goes in v4:
time: 426 us; the launch traced here: 425 us
  Pallas kernels  415 us (97%)
  matrix products  7.55 us (2%)
    pallas_call x2, Pallas kernels, inverse_factor(): pl.pallas_call(inverse_factor_kernel, out_shape=jax.ShapeDtypeStruct((n,...  187 us
    pallas_call x1, Pallas kernels, down_projection(): pl.pallas_call(mlp_kernel, out_shape=(jax.ShapeDtypeStruct((rows, width),...  65.2 us
    pallas_call x1, Pallas kernels, first_image(): pl.pallas_call(first_image_kernel, out_shape=(spread_shape(rows, width),...  58.3 us
    pallas_call x1, Pallas kernels, second_image(): pl.pallas_call(second_image_kernel, out_shape=(jax.ShapeDtypeStruct((RING...  42.4 us
    pallas_call x1, Pallas kernels, gather_kept(): pl.pallas_call(kept_kernel, out_shape=(jax.ShapeDtypeStruct(lead + (width...  34.7 us
    pallas_call x1, Pallas kernels, image_part(): pl.pallas_call(functools.partial(update_kernel, scale), grid=(tile.shape[...  15.6 us
    pallas_call x1, Pallas kernels, image_part(): pl.pallas_call(image_kernel, grid=(tile.shape[0] // height,), out_shape=o...  12.4 us

profile of v4, /device:TPU:1, one launch (start us, length us, event | category | flops | bytes accessed | tf_op | source)
XLA Modules:
  0.0 425.3 jit_solution(5312787585517847499)
XLA Ops:
  0.6 0.0 copy-start.2
  0.6 65.2 %down_projection.1 = (bf16[16,4096]{1,0:T(8,128)(2,1)}, s16[4,2,4,144,512]{4,3,2,1,0:T(8,128)(2,1)}) custom-call(bf16[128,896]{1,0:T(8,128)(2,1)} %hidden_ref.1, bf16[896,4096]{1,0:T(8,128)(2,1)} %weight_ref.1, f32[512,512]{1,0:T(8,128)} %start_ref.1), custom_call_target="tpu_custom_call" | custom-call | tf_op jit(solution)/shard_map/down_projection/pallas_call | solution.py:576
  65.8 0.0 copy-done.2
  65.8 1.7 convolution_convert_fusion.kept_ref
  67.6 34.7 %gather_kept.1 = (bf16[4,4,2,8,4096]{4,3,2,1,0:T(8,128)(2,1)}, bf16[4,4,2,8,512]{4,3,2,1,0:T(8,128)(2,1)}) custom-call(bf16[8,4096]{1,0:T(8,128)(2,1)} %convolution_convert_fusion.kept_ref), custom_call_target="tpu_custom_call" | custom-call | tf_op jit(solution)/shard_map/gather_kept/pallas_call | solution.py:658
  102.3 15.6 %update_image.1 = (f32[4096,512]{1,0:T(8,128)}, f32[512,512]{1,0:T(8,128)}) custom-call(f32[4096,512]{1,0:T(8,128)} %tile_ref.1, s16[4,2,4,144,512]{4,3,2,1,0:T(8,128)(2,1)} %get-tuple-element.15.codes_ref, bf16[256,4096]{1,0:T(8,128)(2,1)} %bitcast.16, bf16[256,512]{1,0:T(8,128)(2,1)} %bitcast.18), custom_call_target="tpu_custom_call" | custom-call | tf_op jit(solution)/shard_map/update_image/pallas_call | solution.py:404
  117.9 58.3 %first_image.1 = (s16[4,2,4,144,512]{4,3,2,1,0:T(8,128)(2,1)}, f32[512,512]{1,0:T(8,128)}) custom-call(f32[512,512]{1,0:T(8,128)} %get-tuple-element.19.part_ref), custom_call_target="tpu_custom_call" | custom-call | tf_op jit(solution)/shard_map/first_image/pallas_call | solution.py:806
  176.2 178.0 %inverse_factor.2.inverse_ref = f32[512,512]{1,0:T(8,128)} custom-call(f32[512,512]{1,0:T(8,128)} %get-tuple-element.21.gram_ref), custom_call_target="tpu_custom_call" | custom-call | flops 8000000000 | bytes 2097152 | tf_op jit(solution)/shard_map/inverse_factor/pallas_call | solution.py:83
  354.2 0.9 convert_convert_fusion
  355.2 2.6 convolution_multiply_fusion.1
  357.8 12.4 %image.1.part_ref = f32[512,512]{1,0:T(8,128)} custom-call(f32[4096,512]{1,0:T(8,128)} %get-tuple-element.29.tile_ref, s16[4,2,4,144,512]{4,3,2,1,0:T(8,128)(2,1)} %get-tuple-element.20.codes_ref), custom_call_target="tpu_custom_call" | custom-call | tf_op jit(solution)/shard_map/image/pallas_call | solution.py:394
  370.2 42.4 %second_image.1 = (f32[4,128,512]{2,1,0:T(8,128)}, f32[512,512]{1,0:T(8,128)}) custom-call(f32[512,512]{1,0:T(8,128)} %image.1.part_ref, f32[512,512]{1,0:T(8,128)} %inverse_factor.2.inverse_ref), custom_call_target="tpu_custom_call" | custom-call | tf_op jit(solution)/shard_map/second_image/pallas_call | solution.py:863
  412.6 0.0 copy-start
  412.6 0.0 copy-start.1
  412.7 8.8 %inverse_factor.3 = f32[512,512]{1,0:T(8,128)} custom-call(f32[512,512]{1,0:T(8,128)} %get-tuple-element.23.gram_ref), custom_call_target="tpu_custom_call" | custom-call | flops 8000000000 | bytes 2097152 | tf_op jit(solution)/shard_map/inverse_factor/pallas_call | solution.py:83
  421.5 0.0 copy-done
  421.5 3.2 convolution_multiply_fusion
  424.7 0.0 copy-done.1
  424.7 0.7 copy.10
  (1 shorter events, 0.0 us)
Async XLA Ops:
  0.6 65.2 %copy-start.2 = (s32[1,8]{1,0:T(1,128)S(1)}, s32[1,8]{1,0:T(1,128)}, u32[]{:S(2)}) copy-start(s32[1,8]{1,0:T(1,128)} %param.8) | copy-start | bytes 100
  412.6 8.8 %copy-start = (f32[4,128,512]{2,1,0:T(8,128)S(1)}, f32[4,128,512]{2,1,0:T(8,128)}, u32[]{:S(2)}) copy-start(f32[4,128,512]{2,1,0:T(8,128)} %get-tuple-element.22) | copy-start | bytes 3145732
  412.6 12.0 %copy-start.1 = (bf16[16,4096]{1,0:T(8,128)(2,1)S(1)}, bf16[16,4096]{1,0:T(8,128)(2,1)}, u32[]{:S(2)}) copy-start(bf16[16,4096]{1,0:T(8,128)(2,1)} %get-tuple-element.28) | copy-start | bytes 393220

commit v5 on v4

--- a/solution.py
+++ b/solution.py
@@ -15,7 +15,9 @@
 HIGH = lax.Precision.HIGH
 
 
-def inverse_factor_kernel(gram_ref, out_ref, scaled, work, state):
+def inverse_factor_kernel(scale, gram_ref, *refs):
+    rows_ref, out_ref = refs[0], refs[-4]
+    scaled, work, state = refs[-3:]
     n = gram_ref.shape[0]
     rows = lax.broadcasted_iota(jnp.int32, (n, n), 0)
     cols = lax.broadcasted_iota(jnp.int32, (n, n), 1)
@@ -75,20 +77,25 @@
             work[...] = work[...] - left * own
             work[pl.ds(j, 1), :] = own
 
-    out_ref[...] = work[...] * row_scale
-
-
-def inverse_factor(gram):
+    inverse = work[...] * row_scale
+    if scale is None:
+        out_ref[...] = inverse
+    else:
+        out_ref[...] = times_transpose(rows_ref[...], inverse, scale)
+
+
+def inverse_factor(gram, rows=None, scale=None):
     n = gram.shape[0]
+    operands = (gram,) if rows is None else (gram, rows)
     return pl.pallas_call(
-        inverse_factor_kernel,
-        out_shape=jax.ShapeDtypeStruct((n, n), F32),
-        in_specs=[pl.BlockSpec(memory_space=pltpu.VMEM)],
+        functools.partial(inverse_factor_kernel, scale),
+        out_shape=jax.ShapeDtypeStruct(operands[-1].shape, F32),
+        in_specs=[pl.BlockSpec(memory_space=pltpu.VMEM)] * len(operands),
         out_specs=pl.BlockSpec(memory_space=pltpu.VMEM),
         scratch_shapes=[pltpu.VMEM((n, n), F32), pltpu.VMEM((n, n), F32), pltpu.SMEM((1,), F32)],
         cost_estimate=pl.CostEstimate(flops=8_000_000_000, bytes_accessed=2 << 20, transcendentals=0),
         name="inverse_factor",
-    )(gram)
+    )(*operands)
 
 
 def times_transpose(rows, factor, scale=1.0):
@@ -315,39 +322,45 @@
     return gather_steps(own, out_ref, by_column, codes.shape[1], links, place)
 
 
-def reduce_y(part_ref, share_ref, relay, build, arrive, links, place):
-    rows, width = share_ref.shape
+HALVES = 2
+
+
+def reduce_steps(part_ref, share_ref, scratch, h, links, place):
+    relay, build, arrive = scratch
+    rows, width = share_ref.shape[0], share_ref.shape[1] // HALVES
     half = width // 2
     low, high = pl.ds(0, half), pl.ds(half, half)
 
-    def quarter(step, cols):
+    def quarter(step, offset, size):
         start = pl.multiple_of(place.along("t", step) * rows, rows)
-        return part_ref.at[pl.ds(start, rows), cols]
+        return part_ref.at[pl.ds(start, rows), pl.ds(h * width + offset, size)]
 
     up, down = place.ahead("t", 1), place.ahead("t", -1)
-    far_up = links.go(quarter(2, low), relay.at[0], up)
-    far_down = links.go(quarter(2, high), relay.at[1], down)
-    near_up = links.go(quarter(1, high), arrive.at[0, :, high], up)
-    near_down = links.go(quarter(-1, low), arrive.at[1, :, low], down)
+    far_up = links.go(quarter(2, 0, half), relay.at[h, 0], up)
+    far_down = links.go(quarter(2, half, half), relay.at[h, 1], down)
+    near_up = links.go(quarter(1, half, half), arrive.at[h, 0, :, high], up)
+    near_down = links.go(quarter(-1, 0, half), arrive.at[h, 1, :, low], down)
+    yield
     far_up.wait_recv()
-    build[0] = quarter(1, low)[...] + relay[0]
-    sum_up = links.go(build.at[0], arrive.at[0, :, low], up)
+    build[h, 0] = quarter(1, 0, half)[...] + relay[h, 0]
+    sum_up = links.go(build.at[h, 0], arrive.at[h, 0, :, low], up)
     far_down.wait_recv()
-    build[1] = quarter(-1, high)[...] + relay[1]
-    sum_down = links.go(build.at[1], arrive.at[1, :, high], down)
+    build[h, 1] = quarter(-1, half, half)[...] + relay[h, 1]
+    sum_down = links.go(build.at[h, 1], arrive.at[h, 1, :, high], down)
+    yield
     for made in (near_up, near_down, sum_up, sum_down):
         made.wait_recv()
-    share_ref[...] = quarter(0, pl.ds(0, width))[...] + (arrive[0] + arrive[1])
-
-
-REDUCE_COPIES = 6
+    share_ref[:, pl.ds(h * width, width)] = quarter(0, 0, width)[...] + (arrive[h, 0] + arrive[h, 1])
+
+
+REDUCE_COPIES = 6 * HALVES
 
 
 def reduce_scratch(rows, width):
     return [
-        pltpu.VMEM((2, rows, width // 2), F32),
-        pltpu.VMEM((2, rows, width // 2), F32),
-        pltpu.VMEM((2, rows, width), F32),
+        pltpu.VMEM((HALVES, 2, rows, width // HALVES // 2), F32),
+        pltpu.VMEM((HALVES, 2, rows, width // HALVES // 2), F32),
+        pltpu.VMEM((HALVES, 2, rows, width // HALVES), F32),
     ]
 
 
@@ -355,23 +368,13 @@
     return [place.ahead("t", 1), place.ahead("t", -1)]
 
 
-def image_block(tile, codes_ref, out_ref):
-    rows = jnp.concatenate([decode(codes_ref[0, 0, i]) for i in range(RING)], axis=0)
-    part = lax.dot_general(
+def image_block(tile, codes):
+    rows = jnp.concatenate(
+        [decode(codes[i, j]) for i in range(codes.shape[0]) for j in range(codes.shape[1])], axis=0
+    )
+    return lax.dot_general(
         tile, rows, (((0,), (0,)), ((), ())), precision=HIGH, preferred_element_type=F32
     )
-
-    @pl.when(pl.program_id(0) == 0)
-    def _():
-        out_ref[...] = part
-
-    @pl.when(pl.program_id(0) > 0)
-    def _():
-        out_ref[...] += part
-
-
-def image_kernel(tile_ref, codes_ref, out_ref):
-    image_block(tile_ref[...], codes_ref, out_ref)
 
 
 def update_kernel(scale, tile_ref, codes_ref, kept_rows_ref, kept_cols_ref, new_ref, out_ref):
@@ -380,48 +383,90 @@
     )
     tile = tile_ref[...] + update * scale
     new_ref[...] = tile
-    image_block(tile, codes_ref, out_ref)
-
-
-def image_part(tile, codes, kept=None, scale=None):
-    width = tile.shape[1]
-    height = RING * (codes.shape[3] - CODE_PAD)
+    part = image_block(tile, codes_ref[0])
+
+    @pl.when(pl.program_id(0) == 0)
+    def _():
+        out_ref[...] = part
+
+    @pl.when(pl.program_id(0) > 0)
+    def _():
+        out_ref[...] += part
+
+
+def update_and_image(tile, codes, kept_rows, kept_cols, scale):
+    width, rank = tile.shape[1], codes.shape[4]
+    tokens = kept_rows.shape[0]
+    height = tile.shape[0] // RING
     tile_spec = pl.BlockSpec((height, width), lambda i: (i, 0))
-    code_spec = pl.BlockSpec((1, 1) + codes.shape[2:], lambda i: (i // 2, i % 2, 0, 0, 0))
-    out_spec = pl.BlockSpec((width, codes.shape[4]), lambda i: (0, 0))
-    out_shape = jax.ShapeDtypeStruct((width, codes.shape[4]), F32)
-    if kept is None:
-        return pl.pallas_call(
-            image_kernel,
-            grid=(tile.shape[0] // height,),
-            out_shape=out_shape,
-            in_specs=[tile_spec, code_spec],
-            out_specs=out_spec,
-            name="image",
-        )(tile, codes)
-    kept_rows, kept_cols = kept
-    tokens = kept_rows.shape[0]
     return pl.pallas_call(
         functools.partial(update_kernel, scale),
-        grid=(tile.shape[0] // height,),
-        out_shape=(jax.ShapeDtypeStruct(tile.shape, F32), out_shape),
+        grid=(RING,),
+        out_shape=(
+            jax.ShapeDtypeStruct(tile.shape, F32),
+            jax.ShapeDtypeStruct((width, rank), F32),
+        ),
         in_specs=[
             tile_spec,
-            code_spec,
+            pl.BlockSpec((1,) + codes.shape[1:], lambda i: (i, 0, 0, 0, 0)),
             pl.BlockSpec((tokens, height), lambda i: (0, i)),
             pl.BlockSpec(kept_cols.shape, lambda i: (0, 0)),
         ],
-        out_specs=(tile_spec, out_spec),
+        out_specs=(tile_spec, pl.BlockSpec((width, rank), lambda i: (0, 0))),
         name="update_image",
     )(tile, codes, kept_rows, kept_cols)
+
+
+def columns_along_y(rows_ref, cols_ref, links, place, sem):
+    width = cols_ref.shape[-1]
+    start = pl.multiple_of((place.x * 2 + place.c) * width, width)
+    source = rows_ref.at[:, :, :, :, pl.ds(start, width)]
+    distance = lax.rem(place.t - place.z + RING, RING)
+    up, down = place.ahead("t", 1), place.ahead("t", -1)
+    to_up = links.copy(source, cols_ref, up)
+    to_down = links.copy(source, cols_ref, down)
+    low = cols_ref.at[pl.ds(0, RING // 2)]
+    high = cols_ref.at[pl.ds(RING // 2, RING // 2)]
+    on_up = links.copy(low, low, up)
+    on_down = links.copy(high, high, down)
+
+    @pl.when(distance == 0)
+    def _():
+        to_up.start()
+        to_down.start()
+        own = pltpu.make_async_copy(source, cols_ref, sem)
+        own.start()
+        own.wait()
+        to_up.wait_send()
+        to_down.wait_send()
+
+    @pl.when(distance == 1)
+    def _():
+        to_up.wait_recv()
+        on_up.start()
+        on_up.wait_send()
+
+    @pl.when(distance == 3)
+    def _():
+        to_down.wait_recv()
+        on_down.start()
+        on_down.wait_send()
+
+    @pl.when(distance == 2)
+    def _():
+        on_up.wait_recv()
+        on_down.wait_recv()
 
 
 def mlp_kernel(
     hidden_ref,
     weight_ref,
     start_ref,
+    keep_ref,
     out_ref,
     spread_ref,
+    rows_ref,
+    cols_ref,
     hid,
     weight,
     part,
@@ -435,14 +480,12 @@
     recv,
     sem,
     swap_sem,
+    cols_sem,
 ):
     place = Place()
     links = Links(send, recv)
     load = pltpu.make_async_copy(weight_ref, weight, sem)
     load.start()
-    share_rows = codes.shape[0] - CODE_PAD
-    share_start = pl.multiple_of(place.t * share_rows, share_rows)
-    encode(start_ref[pl.ds(share_start, share_rows), :], codes)
     meet(plane_neighbours(place) + y_neighbours(place), place)
     tokens = hidden_ref.shape[0]
     width = weight.shape[1]
@@ -451,6 +494,9 @@
     c = place.c
     to_up = links.go(hidden_ref, hid.at[place.t], up)
     to_down = links.go(hidden_ref, hid.at[place.t], down)
+    share_rows = codes.shape[0] - CODE_PAD
+    share_start = pl.multiple_of(place.t * share_rows, share_rows)
+    encode(start_ref[pl.ds(share_start, share_rows), :], codes)
     swap = swap_start(codes, spread_ref, links, place, swap_sem)
     load.wait()
 
@@ -464,9 +510,6 @@
         return links.go(part.at[group, :, 1 - c], pair.at[group], place.other_core())
 
     pairs = [product(place.t, hidden_ref)]
-    swap_end(swap, place)
-    spread = spread_steps(codes, spread_ref, links, place)
-    next(spread)
     below, above, across = place.along("t", -1), place.along("t", 1), place.along("t", 2)
     to_up.wait_recv()
     first = hid.at[below, pl.ds(0, tokens // 2)]
@@ -474,8 +517,9 @@
     to_down.wait_recv()
     second = hid.at[above, pl.ds(tokens // 2, tokens // 2)]
     on_down = links.go(second, second, down)
-    next(spread)
     pairs.append(product(below, hid.at[below]))
+    swap_end(swap, place)
+    spread = spread_steps(codes, spread_ref, links, place)
     next(spread)
     pairs.append(product(above, hid.at[above]))
     on_up.wait_recv()
@@ -489,7 +533,6 @@
         def _(i):
             part[group, i, c] = part[group, i, c] + pair[group, i]
 
-    next(spread)
     ways = ((0, "z", "x"), (1, "x", "z"))
 
     def half_cols(h):
@@ -523,6 +566,7 @@
             early[h, d] = links.go(
                 line(axis, d, piece_cols(h, -d)), near1.at[h, n, :, :, in_half(-d)], place.ahead(axis, d)
             )
+    next(spread)
     for h, axis, _ in ways:
         for n, d in enumerate((1, -1)):
             far[h, d].wait_recv()
@@ -534,6 +578,7 @@
             late[h, d] = links.go(
                 line(axis, d, piece_cols(h, d)), near1.at[h, n, :, :, in_half(d)], place.ahead(axis, d)
             )
+    next(spread)
     for h, axis, other in ways:
         for d in (1, -1):
             early[h, d].wait_recv()
@@ -556,28 +601,44 @@
             late[h, d] = links.go(
                 block(other, d, piece_cols(h, d)), near2.at[h, n, :, in_half(d)], place.ahead(other, d)
             )
+    next(spread)
     for h, axis, other in ways:
         for d in (1, -1):
             early[h, d].wait_recv()
             late[h, d].wait_recv()
         total = block(other, 0, half_cols(h))[...] + (near2[h, 0] + near2[h, 1])
         out_ref[:, half_cols(h)] = total.astype(out_ref.dtype)
+    places = lax.broadcasted_iota(jnp.int32, (out_ref.shape[0], keep_ref.shape[1]), 0)
+    chosen = jnp.where(places == keep_ref[...], 1.0, 0.0).astype(BF16)
+    kept = lax.dot_general(
+        chosen, out_ref[...], (((0,), (0,)), ((), ())), preferred_element_type=F32
+    )
+    rows_ref[place.z, place.x, place.c] = kept.astype(BF16)
+    own = rows_ref.at[by_token(place.z, place.x, place.c)]
+    run(gather_steps(own, rows_ref, by_token, width, links, place))
     run(spread)
     settle(links, place, swap)
-
-
-def down_projection(hidden, weight, start, collective_id):
+    columns_along_y(rows_ref, cols_ref, links, place, cols_sem)
+
+
+def down_projection(hidden, weight, start, keep_index, tile_width, collective_id):
     tokens, depth = hidden.shape
     width = weight.shape[1]
     rows = tokens // (2 * RING)
     share_rows, rank = start.shape[0] // RING, start.shape[1]
-    copies = 32 + 1 + GATHER_COPIES
+    copies = 32 + 1 + 2 * GATHER_COPIES + 4
+    lead = (RING, RING, 2, keep_index.shape[1])
     vmem, anywhere = pl.BlockSpec(memory_space=pltpu.VMEM), pl.BlockSpec(memory_space=pl.ANY)
     return pl.pallas_call(
         mlp_kernel,
-        out_shape=(jax.ShapeDtypeStruct((rows, width), BF16), spread_shape(share_rows, rank)),
-        in_specs=[vmem, anywhere, vmem],
-        out_specs=(vmem, anywhere),
+        out_shape=(
+            jax.ShapeDtypeStruct((rows, width), BF16),
+            spread_shape(share_rows, rank),
+            jax.ShapeDtypeStruct(lead + (width,), BF16),
+            jax.ShapeDtypeStruct(lead + (tile_width,), BF16),
+        ),
+        in_specs=[vmem, anywhere, vmem, vmem],
+        out_specs=(vmem, anywhere, vmem, vmem),
         scratch_shapes=[
             pltpu.VMEM((RING, tokens, depth), BF16),
             pltpu.VMEM((depth, width), BF16),
@@ -592,86 +653,11 @@
             pltpu.SemaphoreType.DMA((copies,)),
             pltpu.SemaphoreType.DMA,
             pltpu.SemaphoreType.DMA,
+            pltpu.SemaphoreType.DMA,
         ],
         compiler_params=pltpu.CompilerParams(collective_id=collective_id, has_side_effects=True),
         name="down_projection",
-    )(hidden, weight, start)
-
-
-def kept_kernel(kept_ref, rows_ref, cols_ref, send, recv, sem):
-    place = Place()
-    links = Links(send, recv)
-    meet(plane_neighbours(place) + y_neighbours(place))
-    local = pltpu.make_async_copy(kept_ref, rows_ref.at[by_token(place.z, place.x, place.c)], sem)
-    local.start()
-    steps = gather_steps(kept_ref, rows_ref, by_token, kept_ref.shape[1], links, place)
-    next(steps)
-    next(steps)
-    local.wait()
-    run(steps)
-    for made in links.started:
-        made.wait_send()
-    width = cols_ref.shape[-1]
-    start = pl.multiple_of((place.x * 2 + place.c) * width, width)
-    source = rows_ref.at[:, :, :, :, pl.ds(start, width)]
-    distance = lax.rem(place.t - place.z + RING, RING)
-    up, down = place.ahead("t", 1), place.ahead("t", -1)
-    to_up = links.copy(source, cols_ref, up)
-    to_down = links.copy(source, cols_ref, down)
-    low = cols_ref.at[pl.ds(0, RING // 2)]
-    high = cols_ref.at[pl.ds(RING // 2, RING // 2)]
-    on_up = links.copy(low, low, up)
-    on_down = links.copy(high, high, down)
-
-    @pl.when(distance == 0)
-    def _():
-        to_up.start()
-        to_down.start()
-        own = pltpu.make_async_copy(source, cols_ref, sem)
-        own.start()
-        own.wait()
-        to_up.wait_send()
-        to_down.wait_send()
-
-    @pl.when(distance == 1)
-    def _():
-        to_up.wait_recv()
-        on_up.start()
-        on_up.wait_send()
-
-    @pl.when(distance == 3)
-    def _():
-        to_down.wait_recv()
-        on_down.start()
-        on_down.wait_send()
-
-    @pl.when(distance == 2)
-    def _():
-        on_up.wait_recv()
-        on_down.wait_recv()
-
-
-def gather_kept(kept, tile_width, collective_id):
-    rows, width = kept.shape
-    lead = (RING, RING, 2, rows)
-    copies = GATHER_COPIES + 4
-    kept_rows, kept_cols = pl.pallas_call(
-        kept_kernel,
-        out_shape=(
-            jax.ShapeDtypeStruct(lead + (width,), kept.dtype),
-            jax.ShapeDtypeStruct(lead + (tile_width,), kept.dtype),
-        ),
-        in_specs=[pl.BlockSpec(memory_space=pltpu.VMEM)],
-        out_specs=(pl.BlockSpec(memory_space=pltpu.VMEM), pl.BlockSpec(memory_space=pltpu.VMEM)),
-        scratch_shapes=[
-            pltpu.SemaphoreType.DMA((copies,)),
-            pltpu.SemaphoreType.DMA((copies,)),
-            pltpu.SemaphoreType.DMA,
-        ],
-        compiler_params=pltpu.CompilerParams(collective_id=collective_id, has_side_effects=True),
-        name="gather_kept",
-    )(kept)
-    return kept_rows.reshape(-1, width), kept_cols.reshape(-1, tile_width)
+    )(hidden, weight, start, keep_index)
 
 
 def total_steps(gram_ref, out_ref, scratch, links, place):
@@ -769,71 +755,110 @@
     )
 
 
-def first_image_kernel(part_ref, out_ref, total_ref, share, gram, codes, *refs):
-    relay, build, arrive = refs[:3]
-    scratch = refs[3:10]
-    send, recv, sem = refs[10:]
+def images_kernel(part_ref, tile_ref, own_ref, share_ref, total_ref, first, gram, codes, every, tile, part, *refs):
+    reduce_one, reduce_two, scratch = refs[:3], refs[3:6], refs[6:13]
+    send, recv, swap_sem, tile_sem = refs[13:]
     place = Place()
     links = Links(send, recv)
+    load = pltpu.make_async_copy(tile_ref, tile, tile_sem)
+    load.start()
     meet(everyone(place), place)
-    reduce_y(part_ref, share, relay, build, arrive, links, place)
-    known = encode(share[...], codes)
-    swap = swap_start(codes, out_ref, links, place, sem)
+    halves = [reduce_steps(part_ref, first, reduce_one, h, links, place) for h in range(HALVES)]
+    for _ in range(2):
+        for half in halves:
+            next(half)
+    for half in halves:
+        run(half)
+    known = encode(first[...], codes)
+    swap = swap_start(codes, every, links, place, swap_sem)
     gram[...] = gram_of(known)
     total = total_steps(gram, total_ref, scratch, links, place)
     next(total)
     swap_end(swap, place)
-    spread = spread_steps(codes, out_ref, links, place)
+    spread = spread_steps(codes, every, links, place)
     next(spread)
     next(total)
     next(spread)
-    next(total)
     next(spread)
     next(total)
     next(total)
+    next(total)
     next(spread)
     next(total)
     next(spread)
+    load.wait()
+    run(spread)
+    index = (place.z * RING + place.x) * 2 + place.c
+    own_ref[...] = every[lax.div(index, 2 * RING), lax.rem(lax.div(index, RING), 2), lax.rem(index, RING)]
+    height = tile.shape[0] // RING
+    width = part.shape[1] // HALVES
+
+    def product(h):
+        cols = pl.ds(h * width, width)
+        part[:, cols] = jnp.zeros((part.shape[0], width), F32)
+
+        @pl.loop(0, RING)
+        def _(i):
+            rows = tile[pl.ds(pl.multiple_of(i * height, height), height), :]
+            part[:, cols] = part[:, cols] + image_block(rows, every[i, :, :, :, cols])
+
+    halves = [reduce_steps(part, share_ref, reduce_two, h, links, place) for h in range(HALVES)]
+    product(0)
+    next(halves[0])
+    next(total)
+    product(1)
+    next(halves[1])
+    next(halves[0])
     run(total)
-    run(spread)
+    next(halves[1])
+    for half in halves:
+        run(half)
     settle(links, place, swap)
 
 
-def first_image(part, collective_id):
+def images(part, tile, collective_id):
     rows, width = part.shape[0] // RING, part.shape[1]
-    copies = REDUCE_COPIES + 1 + GATHER_COPIES + TOTAL_COPIES
-    vmem = pl.BlockSpec(memory_space=pltpu.VMEM)
+    copies = 2 * REDUCE_COPIES + 1 + GATHER_COPIES + TOTAL_COPIES
+    vmem, anywhere = pl.BlockSpec(memory_space=pltpu.VMEM), pl.BlockSpec(memory_space=pl.ANY)
+    coded = spread_shape(rows, width)
     return pl.pallas_call(
-        first_image_kernel,
-        out_shape=(spread_shape(rows, width), jax.ShapeDtypeStruct((width, width), F32)),
-        in_specs=[vmem],
-        out_specs=(pl.BlockSpec(memory_space=pl.ANY), vmem),
+        images_kernel,
+        out_shape=(
+            jax.ShapeDtypeStruct(coded.shape[3:], coded.dtype),
+            jax.ShapeDtypeStruct((rows, width), F32),
+            jax.ShapeDtypeStruct((width, width), F32),
+        ),
+        in_specs=[vmem, anywhere],
+        out_specs=(vmem, vmem, vmem),
         scratch_shapes=[
             pltpu.VMEM((rows, width), F32),
             pltpu.VMEM((width, width), F32),
-            pltpu.VMEM((rows + CODE_PAD, width), jnp.int16),
+            pltpu.VMEM(coded.shape[3:], coded.dtype),
+            pltpu.VMEM(coded.shape, coded.dtype),
+            pltpu.VMEM(tile.shape, F32),
+            pltpu.VMEM(part.shape, F32),
         ]
+        + reduce_scratch(rows, width)
         + reduce_scratch(rows, width)
         + total_scratch(width)
         + [
             pltpu.SemaphoreType.DMA((copies,)),
             pltpu.SemaphoreType.DMA((copies,)),
             pltpu.SemaphoreType.DMA,
+            pltpu.SemaphoreType.DMA,
         ],
         compiler_params=pltpu.CompilerParams(collective_id=collective_id, has_side_effects=True),
-        name="first_image",
-    )(part)
-
-
-def second_image_kernel(part_ref, inverse_ref, rows_ref, total_ref, share, gram, *refs):
-    relay, build, arrive = refs[:3]
-    scratch = refs[3:10]
-    send, recv = refs[10:]
+        name="images",
+    )(part, tile)
+
+
+def bases_kernel(scale, share_ref, own_ref, inverse_ref, rows_ref, total_ref, basis_ref, gram, *refs):
+    scratch = refs[:7]
+    send, recv = refs[7:]
     place = Place()
     links = Links(send, recv)
     meet(everyone(place))
-    reduce_y(part_ref, share, relay, build, arrive, links, place)
-    image = times_transpose(share[...], inverse_ref[...])
+    image = times_transpose(share_ref[...], inverse_ref[...])
     rows_ref[pl.ds(place.t, 1)] = image[None]
     gram[...] = gram_of(image)
     total = total_steps(gram, total_ref, scratch, links, place)
@@ -841,6 +866,7 @@
     next(total)
     own = rows_ref.at[place.t]
     around = [links.go(own, own, place.ahead("t", d)) for d in (1, -1)]
+    basis_ref[...] = times_transpose(decode(own_ref[...]), inverse_ref[...], scale)
     next(total)
     next(total)
     next(total)
@@ -856,49 +882,43 @@
     settle(links, place)
 
 
-def second_image(part, inverse, collective_id):
-    rows, width = part.shape[0] // RING, part.shape[1]
-    copies = REDUCE_COPIES + TOTAL_COPIES + 4
+def bases(share, own, inverse, scale, collective_id):
+    rows, width = share.shape
+    copies = TOTAL_COPIES + 4
     vmem = pl.BlockSpec(memory_space=pltpu.VMEM)
-    out, total = pl.pallas_call(
-        second_image_kernel,
+    out, total, basis = pl.pallas_call(
+        functools.partial(bases_kernel, scale),
         out_shape=(
             jax.ShapeDtypeStruct((RING, rows, width), F32),
             jax.ShapeDtypeStruct((width, width), F32),
+            jax.ShapeDtypeStruct((rows, width), F32),
         ),
-        in_specs=[vmem, vmem],
-        out_specs=(vmem, vmem),
-        scratch_shapes=[pltpu.VMEM((rows, width), F32), pltpu.VMEM((width, width), F32)]
-        + reduce_scratch(rows, width)
+        in_specs=[vmem] * 3,
+        out_specs=(vmem, vmem, vmem),
+        scratch_shapes=[pltpu.VMEM((width, width), F32)]
         + total_scratch(width)
         + [pltpu.SemaphoreType.DMA((copies,)), pltpu.SemaphoreType.DMA((copies,))],
         compiler_params=pltpu.CompilerParams(collective_id=collective_id, has_side_effects=True),
-        name="second_image",
-    )(part, inverse)
-    return out.reshape(-1, width), total
+        name="bases",
+    )(share, own, inverse)
+    return out.reshape(-1, width), total, basis
 
 
 def body(hidden, down_weight, covariance, keep_index, start_basis):
-    fsdp_count = lax.axis_size("fsdp")
-    total_tokens = TOK_DEV * fsdp_count
-    block_width = covariance.shape[1]
-    f = lax.axis_index("fsdp")
+    total_tokens = TOK_DEV * lax.axis_size("fsdp")
     root = math.sqrt(D)
-
-    mlp_out, start_codes = down_projection(hidden, down_weight, start_basis, 0)
-    listed = keep_index[0]
-    positions = jnp.arange(mlp_out.shape[0], dtype=jnp.int32)
-    chosen = (listed[:, None] == positions[None, :]).astype(BF16)
-    kept = jnp.dot(chosen, mlp_out, preferred_element_type=F32).astype(BF16)
-    kept_pair = gather_kept(kept, block_width, 2)
-    new_covariance, part_one = image_part(covariance, start_codes, kept_pair, 1.0 / total_tokens)
-    codes_one, total_one = first_image(part_one, 1)
+    mlp_out, start_codes, kept_rows, kept_cols = down_projection(
+        hidden, down_weight, start_basis, keep_index, covariance.shape[1], 0
+    )
+    kept_rows = kept_rows.reshape(-1, kept_rows.shape[-1])
+    kept_cols = kept_cols.reshape(-1, kept_cols.shape[-1])
+    new_covariance, part_one = update_and_image(
+        covariance, start_codes, kept_rows, kept_cols, 1.0 / total_tokens
+    )
+    own_codes, share_two, total_one = images(part_one, new_covariance, 1)
     inverse_one = inverse_factor(total_one)
-    every = codes_one.reshape(fsdp_count, -1, codes_one.shape[-1])
-    own_rows = decode(lax.dynamic_index_in_dim(every, f, 0, keepdims=False))
-    first_basis = times_transpose(own_rows, inverse_one, root)
-    whole_two, total_two = second_image(image_part(new_covariance, codes_one), inverse_one, 3)
-    final_basis = times_transpose(whole_two, inverse_factor(total_two), root)
+    rows_two, total_two, first_basis = bases(share_two, own_codes, inverse_one, root, 2)
+    final_basis = inverse_factor(total_two, rows_two, root)
     return (mlp_out, new_covariance, first_basis, final_basis)
 
 

time: 426 us -> 401 us (0.941)
  Pallas kernels: 415 us -> 399 us
  matrix products: 7.55 us -> 0 us
    pallas_call x7 -> x5, Pallas kernels: 350 us -> 308 us  [the longest x2 188 us: inverse_factor(): pl.pallas_call(functools.partial(inverse_factor_kernel, scale), out_shape...]
    pallas_call x1, Pallas kernels: 65.2 us -> 91 us  [down_projection(): pl.pallas_call(mlp_kernel, out_shape=(jax.ShapeDtypeStruct((rows, width),...]
    dot_general x3 -> x0, matrix products: 7.55 us -> none  [the longest x2 5.8 us: times_transpose(): lax.dot_general(rows, factor, (((1,), (1,)), ((), ())), precision=HIGH, p...]
where the time goes in v5:
time: 401 us
  Pallas kernels  399 us (100%)
    pallas_call x2, Pallas kernels, inverse_factor(): pl.pallas_call(functools.partial(inverse_factor_kernel, scale), out_shape...  188 us
    pallas_call x1, Pallas kernels, down_projection(): pl.pallas_call(mlp_kernel, out_shape=(jax.ShapeDtypeStruct((rows, width),...  91 us
    pallas_call x1, Pallas kernels, images(): pl.pallas_call(images_kernel, out_shape=(jax.ShapeDtypeStruct(coded.shape...  74.4 us
    pallas_call x1, Pallas kernels, bases(): pl.pallas_call(functools.partial(bases_kernel, scale), out_shape=(jax.Sha...  31.8 us
    pallas_call x1, Pallas kernels, update_and_image(): pl.pallas_call(functools.partial(update_kernel, scale), grid=(RING,), out...  13.8 us

profile of v5, /device:TPU:1, one launch (start us, length us, event | category | flops | bytes accessed | tf_op | source)
XLA Modules:
  0.0 401.0 jit_solution(511228644685061974)
XLA Ops:
  0.6 91.0 %down_projection.1 = (bf16[16,4096]{1,0:T(8,128)(2,1)}, s16[4,2,4,144,512]{4,3,2,1,0:T(8,128)(2,1)}, bf16[4,4,2,8,4096]{4,3,2,1,0:T(8,128)(2,1)}, bf16[4,4,2,8,512]{4,3,2,1,0:T(8,128)(2,1)}) custom-call(bf16[128,896]{1,0:T(8,128)(2,1)} %hidden_ref.1, bf16[896,4096]{1,0:T(8,128)(2,1)} %weight_ref.1, f32[512,512]{1,0:T(8,128)} %start_ref.1, s32[1,8]{1,0:T(1,128)} %keep_ref.1), custom_call_target="tpu_custom_call" | custom-call | tf_op jit(solution)/shard_map/down_projection/pallas_call | solution.py:632
  91.6 13.8 %update_image.1 = (f32[4096,512]{1,0:T(8,128)}, f32[512,512]{1,0:T(8,128)}) custom-call(f32[4096,512]{1,0:T(8,128)} %tile_ref.1, s16[4,2,4,144,512]{4,3,2,1,0:T(8,128)(2,1)} %get-tuple-element.17.codes_ref, bf16[256,4096]{1,0:T(8,128)(2,1)} %bitcast.3, bf16[256,512]{1,0:T(8,128)(2,1)} %bitcast.4), custom_call_target="tpu_custom_call" | custom-call | tf_op jit(solution)/shard_map/update_image/pallas_call | solution.py:402
  105.4 74.4 %images.1 = (s16[144,512]{1,0:T(8,128)(2,1)}, f32[128,512]{1,0:T(8,128)}, f32[512,512]{1,0:T(8,128)}) custom-call(f32[512,512]{1,0:T(8,128)} %get-tuple-element.21.part_ref, f32[4096,512]{1,0:T(8,128)} %get-tuple-element.33.tile_ref), custom_call_target="tpu_custom_call" | custom-call | tf_op jit(solution)/shard_map/images/pallas_call | solution.py:824
  179.8 178.0 %inverse_factor.2.inverse_ref = f32[512,512]{1,0:T(8,128)} custom-call(f32[512,512]{1,0:T(8,128)} %get-tuple-element.24.gram_ref), custom_call_target="tpu_custom_call" | custom-call | flops 8000000000 | bytes 2097152 | tf_op jit(solution)/shard_map/inverse_factor/pallas_call | solution.py:90
  357.8 31.8 %bases.1 = (f32[4,128,512]{2,1,0:T(8,128)}, f32[512,512]{1,0:T(8,128)}, f32[128,512]{1,0:T(8,128)}) custom-call(f32[128,512]{1,0:T(8,128)} %get-tuple-element.22.share_ref, s16[144,512]{1,0:T(8,128)(2,1)} %get-tuple-element.23.own_ref, f32[512,512]{1,0:T(8,128)} %inverse_factor.2.inverse_ref), custom_call_target="tpu_custom_call" | custom-call | tf_op jit(solution)/shard_map/bases/pallas_call | solution.py:889
  389.6 0.0 copy-start.1
  389.6 0.0 copy-start
  389.6 10.0 %inverse_factor.3 = f32[512,512]{1,0:T(8,128)} custom-call(f32[512,512]{1,0:T(8,128)} %get-tuple-element.26.gram_ref, f32[512,512]{1,0:T(8,128)} %bitcast.5), custom_call_target="tpu_custom_call" | custom-call | flops 8000000000 | bytes 2097152 | tf_op jit(solution)/shard_map/inverse_factor/pallas_call | solution.py:90
  399.7 0.0 copy-done.1
  399.7 0.7 copy.11
  400.3 0.0 copy-done
  400.3 0.7 copy.12
Async XLA Ops:
  389.6 10.0 %copy-start.1 = (bf16[16,4096]{1,0:T(8,128)(2,1)S(1)}, bf16[16,4096]{1,0:T(8,128)(2,1)}, u32[]{:S(2)}) copy-start(bf16[16,4096]{1,0:T(8,128)(2,1)} %get-tuple-element.32) | copy-start | bytes 393220
  389.6 10.7 %copy-start = (f32[128,512]{1,0:T(8,128)S(1)}, f32[128,512]{1,0:T(8,128)}, u32[]{:S(2)}) copy-start(f32[128,512]{1,0:T(8,128)} %get-tuple-element.34) | copy-start | bytes 786436
